TPU v7x, 32 devices: a whole 2x2x4 slice. The times are simulated.
32 devices in a mesh: dp: 4 (over z), ctx: 4 (over y, x), tensor: 2 (over core).
Axes of the slice: x: 2, y: 2, z: 4, core: 2. Of those that a mesh axis runs over, the one named last changes fastest.
Arguments:
- tokens: bfloat16 [12, 1024, 768], P('dp', 'ctx'), may hold values from -6 to 6
- segment_ids: int32 [12, 1024], P('dp', 'ctx'), may hold values from 0 to 3, never falling along the last dimension, each value on 1 to 512 neighbouring positions
- w_qkv: bfloat16 [3, 768, 768], P(None, None, 'tensor'), may hold values from -0.21875 to 0.21875
- w_out: bfloat16 [768, 768], P('tensor'), may hold values from -3 to 3
- w_up: bfloat16 [3072, 768], P('tensor'), may hold values from -0.21875 to 0.21875
- w_down: bfloat16 [3072, 768], P('tensor'), may hold values from -0.109375 to 0.109375
- norm_gain: float32 [2, 768], replicated, may hold values from 0.1 to 1.9
- norm_bias: float32 [2, 768], replicated, may hold values from -1.5 to 1.5
- grad_out: bfloat16 [12, 1024, 768], P('dp', 'ctx'), may hold values from -6 to 6
Outputs:
- out: bfloat16 [12, 1024, 768], P('dp', 'ctx')
- grad_tokens: float32 [12, 1024, 768], P('dp', 'ctx')
- grad_qkv: float32 [3, 768, 768], P(None, 'ctx', 'tensor')
- grad_w_out: float32 [768, 768], P('tensor', 'ctx')
- grad_up: float32 [3072, 768], P('tensor', 'ctx')
- grad_down: float32 [3072, 768], P('tensor', 'ctx')
- grad_gain: float32 [2, 768], P(None, 'ctx')
- grad_bias: float32 [2, 768], P(None, 'ctx')
Inputs may be any that keep to these rules, and one draw needn't show every extreme that they name: `segment_ids`: documents are contiguous runs of equal ids that never fall along a sequence; each id names 1 to 512 tokens and one document has exactly 512.
All inputs are finite; a program needn't handle non-finite values.
Results may differ from a plain program's by a relative error of at most 0.02.
Values may be sent and summed in bfloat16 or wider, within the bound.
No kernel may reach another device: no remote copies, remote signals or barrier semaphores. Data moves between devices by JAX's collectives and lax.ppermute only.
A program may use at most 320 MiB of HBM per device.

v0:
```python
import functools
import jax
import jax.numpy as jnp
from jax import lax
from jax.experimental import pallas as pl
from jax.experimental.pallas import tpu as pltpu
from jax.sharding import PartitionSpec as P

HEAD_DIM = 64
LANES = 128
STAT_ROWS = 16
BIG = 2.0**30
low, full = jnp.bfloat16, jnp.float32


def dot_nn(left, right):
    return lax.dot_general(left, right, (((1,), (0,)), ((), ())), preferred_element_type=full)


def dot_nt(left, right):
    return lax.dot_general(left, right, (((1,), (1,)), ((), ())), preferred_element_type=full)


def dot_tn(left, right):
    return lax.dot_general(left, right, (((0,), (0,)), ((), ())), preferred_element_type=full)


def two_parts(values):
    high = values.astype(low)
    return high, (values - high.astype(full)).astype(low)


def project_kernel(w_qkv, part_a, part_b, out):
    half = part_a.shape[2] - STAT_ROWS
    local = w_qkv.shape[2]
    rows = jnp.concatenate([part[0, 0, :half, :] for part in (part_a, part_b)], axis=0)
    for kind in range(3):
        product = dot_nn(rows, w_qkv[kind])
        if kind == 0:
            product = product * 0.125
        out[0, 0, :, kind * local : (kind + 1) * local] = product.astype(low)
    ids = lax.broadcasted_iota(jnp.int32, (LANES, half), 0).astype(full)
    for which, part in enumerate((part_a, part_b)):
        row = part[0, 0, half : half + 1, :half].astype(full)
        out[0, 0, which * half : (which + 1) * half, 3 * local :] = jnp.where(ids == row, 1.0, 0.0).T.astype(low)


class Lanes:
    def __init__(self, heads):
        self.local = heads * HEAD_DIM

    def of(self, kind, pair):
        start = kind * self.local + pair * LANES
        return slice(start, start + LANES)

    @property
    def hot(self):
        return slice(3 * self.local, 3 * self.local + LANES)


def split_heads(value):
    left = lax.broadcasted_iota(jnp.int32, value.shape, 1) < HEAD_DIM
    zero = jnp.zeros_like(value)
    return jnp.where(left, value, zero), jnp.where(left, zero, value)


def present(hot):
    return jnp.max(hot.astype(full), axis=0, keepdims=True)


def over_units(counts, unit_refs, lanes, own_ids, body):
    flags = [
        jnp.max(own_ids * present(ref[0, 0, :, lanes.hot])) > 0.0 if count == 1 else None
        for count, ref in zip(counts, unit_refs)
    ]
    for number, (count, ref) in enumerate(zip(counts, unit_refs)):
        if count == 1:
            pl.when(flags[number])(functools.partial(body, number, 0))
        else:

            def step(index, carry, number=number, ref=ref):
                shared = jnp.max(own_ids * present(ref[0, index, :, lanes.hot])) > 0.0
                pl.when(shared)(functools.partial(body, number, index))
                return carry

            lax.fori_loop(0, count, step, 0)


def attend_kernel(counts, heads, begin, finish, *refs):
    lanes, pairs, units = Lanes(heads), heads // 2, len(counts)
    own, unit_refs = refs[0], refs[1 : 1 + units]
    refs = refs[1 + units :]
    if not begin:
        acc_in, stat_in = refs[:2]
        refs = refs[2:]
    if finish:
        mixed_keep, mixed_send, lse_out = refs[:3]
        refs = refs[3:]
    else:
        acc_out, stat_out = refs[:2]
        refs = refs[2:]
    q_aug, scores, weights, stat, acc = refs
    span = own.shape[2]
    half = span // 2
    hot_own = own[0, 0, :, lanes.hot]
    penalty = ((hot_own.astype(full) - 1.0) * BIG).astype(low)
    for pair in range(pairs):
        for side, masked in enumerate(split_heads(own[0, 0, :, lanes.of(0, pair)])):
            q_aug[2 * pair + side] = jnp.concatenate([masked, penalty], axis=1)
    if not begin:
        acc[...] = acc_in[0]
        stat[...] = stat_in[0]

    def block(ref, index, first):
        hot = ref[0, index, :, lanes.hot]
        peaks = []
        for pair in range(pairs):
            k_aug = jnp.concatenate([ref[0, index, :, lanes.of(1, pair)], hot], axis=1)
            for side in range(2):
                head = 2 * pair + side
                product = dot_nt(k_aug, q_aug[head])
                scores[head] = product
                peak = jnp.max(product, axis=0, keepdims=True)
                peaks.append(peak if first else jnp.maximum(peak, stat[head : head + 1, :]))
        sums = []
        for head in range(heads):
            weight = jnp.exp(scores[head] - peaks[head])
            sums.append(jnp.sum(weight, axis=0, keepdims=True))
            weights[head] = weight.astype(low)
        for pair in range(pairs):
            turned = ref[0, index, :, lanes.of(2, pair)].T
            for side in range(2):
                head = 2 * pair + side
                rows = slice(head * HEAD_DIM, (head + 1) * HEAD_DIM)
                mix = dot_nn(turned[side * HEAD_DIM : (side + 1) * HEAD_DIM], weights[head])
                total = sums[head]
                if not first:
                    shrink = jnp.exp(stat[head : head + 1, :] - peaks[head])
                    total = total + stat[8 + head : 9 + head, :] * shrink
                    mix = mix + acc[rows, :] * shrink
                acc[rows, :] = mix
                stat[head : head + 1, :] = peaks[head]
                stat[8 + head : 9 + head, :] = total

    if begin:
        block(own, 0, True)
    over_units(
        counts, unit_refs, lanes, present(hot_own), lambda number, index: block(unit_refs[number], index, False)
    )
    if not finish:
        acc_out[0] = acc[...]
        stat_out[0] = stat[...]
        return
    totals = stat[8 : 8 + heads, :]
    lse = stat[0:heads, :] + jnp.log(totals)
    lse_out[0, 0:heads, :] = lse
    lse_out[0, heads:8, :] = jnp.zeros((8 - heads, span), full)
    scale = 1.0 / totals
    for pair in range(pairs):
        chosen = slice(pair * LANES, (pair + 1) * LANES)
        mixed = jnp.concatenate(
            [
                acc[head * HEAD_DIM : (head + 1) * HEAD_DIM, :] * scale[head : head + 1, :]
                for head in (2 * pair, 2 * pair + 1)
            ],
            axis=0,
        ).T.astype(low)
        mixed_keep[0, :, chosen] = mixed[:half]
        mixed_send[0, :half, chosen] = mixed[half:]
    row_of = lax.broadcasted_iota(jnp.int32, (STAT_ROWS, half), 0)
    for column in range(pairs):
        tile = jnp.zeros((STAT_ROWS, half), full)
        for which in range(2):
            row = lse[which * pairs + column : which * pairs + column + 1, half:]
            for kind, part in enumerate(two_parts(row)):
                tile = jnp.where(row_of == kind + 2 * which, part.astype(full), tile)
        mixed_send[0, half:, column * LANES : (column + 1) * LANES] = tile.astype(low)


def stat_row(grad_a, grad_b, at, kind, head, half):
    tile = slice(head * LANES, (head + 1) * LANES)
    parts = []
    for other, ref in enumerate((grad_a, grad_b)):
        row = half + 2 * kind + 4 * other
        parts.append(
            ref[at + (slice(row, row + 1), tile)].astype(full)
            + ref[at + (slice(row + 1, row + 2), tile)].astype(full)
        )
    return jnp.concatenate(parts, axis=1)


def query_grad_kernel(counts, heads, *refs):
    lanes, pairs, units = Lanes(heads), heads // 2, len(counts)
    own, grad_a, grad_b, w_out = refs[:4]
    unit_refs = refs[4 : 4 + units]
    dq_out, dk_out, dv_out, q_aug, d_mix, rows_of, scores, weights, d_scores, acc = refs[4 + units :]
    span = own.shape[2]
    half = span // 2
    hot_own = own[0, 0, :, lanes.hot]
    penalty = ((hot_own.astype(full) - 1.0) * BIG).astype(low)
    d_attn = jnp.concatenate([grad_a[0, :half, :], grad_b[0, :half, :]], axis=0)
    d_mixed = dot_nt(d_attn, w_out[...]).astype(low)
    for pair in range(pairs):
        q_parts = split_heads(own[0, 0, :, lanes.of(0, pair)])
        d_parts = split_heads(d_mixed[:, pair * LANES : (pair + 1) * LANES])
        for side in range(2):
            head = 2 * pair + side
            q_aug[head] = jnp.concatenate([q_parts[side], penalty], axis=1)
            d_mix[head] = d_parts[side]
            rows_of[head : head + 1, :] = stat_row(grad_a, grad_b, (0,), 0, head, half)
            rows_of[8 + head : 9 + head, :] = stat_row(grad_a, grad_b, (0,), 1, head, half)

    def block(ref, index, first):
        hot = ref[0, index, :, lanes.hot]
        for pair in range(pairs):
            k_aug = jnp.concatenate([ref[0, index, :, lanes.of(1, pair)], hot], axis=1)
            for side in range(2):
                head = 2 * pair + side
                scores[head] = dot_nt(k_aug, q_aug[head])
        for pair in range(pairs):
            values = ref[0, index, :, lanes.of(2, pair)]
            for side in range(2):
                head = 2 * pair + side
                weight = jnp.exp(scores[head] - rows_of[head : head + 1, :])
                d_weight = dot_nt(values, d_mix[head])
                d_scores[head] = (weight * (d_weight - rows_of[8 + head : 9 + head, :])).astype(low)
                if first:
                    weights[head] = weight.astype(low)
        for pair in range(pairs):
            turned = ref[0, index, :, lanes.of(1, pair)].T
            for side in range(2):
                head = 2 * pair + side
                rows = slice(head * HEAD_DIM, (head + 1) * HEAD_DIM)
                product = dot_nn(turned[side * HEAD_DIM : (side + 1) * HEAD_DIM], d_scores[head])
                acc[rows, :] = product if first else acc[rows, :] + product
            if first:
                chosen = slice(pair * LANES, (pair + 1) * LANES)
                one, two = 2 * pair, 2 * pair + 1
                dv_out[0, :, chosen] = dot_nn(weights[one], d_mix[one]) + dot_nn(weights[two], d_mix[two])
                dk_out[0, :, chosen] = dot_nn(d_scores[one], q_aug[one, :, :LANES]) + dot_nn(
                    d_scores[two], q_aug[two, :, :LANES]
                )

    block(own, 0, True)
    over_units(
        counts, unit_refs, lanes, present(hot_own), lambda number, index: block(unit_refs[number], index, False)
    )
    for pair in range(pairs):
        chosen = slice(pair * LANES, (pair + 1) * LANES)
        dq_out[0, :, chosen] = (acc[chosen, :] * 0.125).T.astype(low)


def key_grad_kernel(counts, heads, turn_ref, *refs):
    lanes, pairs, units = Lanes(heads), heads // 2, len(counts)
    own, dq_in, dk_in, dv_in, w_out, w_qkv = refs[:6]
    unit_refs = refs[6 : 6 + units]
    a_refs = refs[6 + units : 6 + 2 * units]
    b_refs = refs[6 + 2 * units : 6 + 3 * units]
    d_kv, d_input, k_aug, q_mask, d_mix, scores, weights, d_scores, dk_acc, dv_acc = refs[6 + 3 * units :]
    span = own.shape[2]
    half = span // 2
    local = lanes.local
    turn = turn_ref[0]
    hot_own = own[0, 0, :, lanes.hot]
    for pair in range(pairs):
        k_aug[pair] = jnp.concatenate([own[0, 0, :, lanes.of(1, pair)], hot_own], axis=1)
    dk_acc[...] = dk_in[0]
    dv_acc[...] = dv_in[0]

    def block(number, index):
        ref, grad_a, grad_b = unit_refs[number], a_refs[number], b_refs[number]
        penalty = ((ref[0, index, :, lanes.hot].astype(full) - 1.0) * BIG).astype(low)
        d_attn = jnp.concatenate([grad_a[0, index, :half, :], grad_b[0, index, :half, :]], axis=0)
        d_mixed = dot_nt(d_attn, w_out[...]).astype(low)
        for pair in range(pairs):
            q_parts = split_heads(ref[0, index, :, lanes.of(0, pair)])
            d_parts = split_heads(d_mixed[:, pair * LANES : (pair + 1) * LANES])
            for side in range(2):
                head = 2 * pair + side
                q_mask[head] = q_parts[side]
                d_mix[head] = d_parts[side]
                scores[head] = dot_nt(k_aug[pair], jnp.concatenate([q_parts[side], penalty], axis=1))
        for pair in range(pairs):
            values = own[0, 0, :, lanes.of(2, pair)]
            for side in range(2):
                head = 2 * pair + side
                lse = stat_row(grad_a, grad_b, (0, index), 0, head, half)
                delta = stat_row(grad_a, grad_b, (0, index), 1, head, half)
                weight = jnp.exp(scores[head] - lse)
                d_weight = dot_nt(values, d_mix[head])
                d_scores[head] = (weight * (d_weight - delta)).astype(low)
                weights[head] = weight.astype(low)
        for pair in range(pairs):
            chosen = slice(pair * LANES, (pair + 1) * LANES)
            one, two = 2 * pair, 2 * pair + 1
            dv_acc[:, chosen] += dot_nn(weights[one], d_mix[one]) + dot_nn(weights[two], d_mix[two])
            dk_acc[:, chosen] += dot_nn(d_scores[one], q_mask[one]) + dot_nn(d_scores[two], q_mask[two])

    over_units(counts, unit_refs, lanes, present(hot_own), block)
    half_a = pl.ds(pl.multiple_of(turn * half, half), half)
    half_b = pl.ds(pl.multiple_of((1 - turn) * half, half), half)
    for kind, value in enumerate((dq_in[0], dk_acc[...].astype(low), dv_acc[...].astype(low))):
        chosen = slice(kind * local, (kind + 1) * local)
        product = dot_nt(value, w_qkv[kind])
        total = product if kind == 0 else total + product
        if kind > 0:
            d_kv[0, :, (kind - 1) * local : kind * local] = value
    total = total.astype(low)
    d_input[0, half_a, :] = total[:half]
    d_input[0, half_b, :] = total[half:]


def padded(block):
    return -(-block // 16) * 16


def lane_part(ref, half=None):
    if half is None:
        return lambda lanes: ref[:, lanes]
    return lambda lanes: ref[:, :half, lanes].reshape(ref.shape[0] * half, LANES)


def put_slots(turned, slots, values, owners, block):
    def turn_lanes(step, carry):
        lanes = pl.ds(pl.multiple_of(step * LANES, LANES), LANES)
        start = 0
        for load in values:
            value = load(lanes)
            turned[lanes, start : start + value.shape[0]] = value.astype(turned.dtype).T
            start += value.shape[0]
        return carry

    lax.fori_loop(0, turned.shape[0] // LANES, turn_lanes, 0)
    room = padded(block)
    for slot in range(slots.shape[0] // room):
        source = pl.ds(pl.multiple_of(owners[slot] * block, 16 if block % 16 == 0 else 8), block)
        slots[slot * room : slot * room + block, :] = turned[source, :].astype(low)


def places_of(targets):
    return [(ref, index) for ref in targets for index in range(ref.shape[0])]


def put_blocks(product, targets, block, skip):
    for slot, (ref, index) in enumerate(places_of(targets)):
        start = slot * padded(block)
        ref[index, skip : skip + block, :] = product[start : start + block].astype(low)


def pair_grad_kernel(owners, left_a, left_b, right_a, right_b, *refs):
    targets, (turned, slots) = refs[:-2], refs[-2:]
    block = targets[0].shape[1]

    @pl.when(pl.program_id(0) == 0)
    def _():
        put_slots(turned, slots, [lane_part(part) for part in (left_a, left_b)], owners, block)

    right = jnp.concatenate([right_a[...], right_b[...]], axis=0)
    put_blocks(dot_nn(slots[...], right), targets, block, 0)


def half_rows(part, half):
    return part[:, :half, :].reshape(part.shape[0] * half, -1)


def both_rows(value, half):
    return jnp.concatenate([half_rows(value[:, :half], half), half_rows(value[:, half:], half)], axis=0)


def query_out_grad_kernel(owners, tok_a, tok_b, d_query, d_attn_a, d_attn_b, mixed_a, mixed_b, small, *refs):
    targets, (turned, slots, turned_second, slots_second) = refs[:-4], refs[-4:]
    span, local = d_query.shape[1:]
    half = span // 2
    block = targets[0].shape[1] - STAT_ROWS
    put_slots(turned, slots, [lane_part(part, half) for part in (tok_a, tok_b)], owners, block)
    first = dot_nn(slots[...], both_rows(d_query, half)).astype(low)
    put_slots(turned_second, slots_second, [lane_part(part, half) for part in (d_attn_a, d_attn_b)], owners, block)
    mixed = jnp.concatenate([half_rows(part, half) for part in (mixed_a, mixed_b)], axis=0)
    second = dot_nn(slots_second[...], mixed).astype(low)
    for slot, (ref, index) in enumerate(places_of(targets)):
        start = slot * padded(block)
        for which, product in enumerate((first, second)):
            columns = slice(which * local, (which + 1) * local)
            ref[index, STAT_ROWS:, columns] = product[start : start + block]
        ref[index, :STAT_ROWS, :local] = jnp.zeros((STAT_ROWS, local), low)
        ref[index, :STAT_ROWS, local:] = small[owners[slot]].astype(low)


def key_value_grad_kernel(owners, tok_a, tok_b, d_kv, *refs):
    targets, (turned, slots) = refs[:-2], refs[-2:]
    half = d_kv.shape[1] // 2
    block = targets[0].shape[1]
    put_slots(turned, slots, [lane_part(part, half) for part in (tok_a, tok_b)], owners, block)
    put_blocks(dot_nn(slots[...], both_rows(d_kv, half)), targets, block, 0)


def norm_of(residual):
    center = residual - jnp.mean(residual, axis=-1, keepdims=True)
    inverse = lax.rsqrt(jnp.mean(center * center, axis=-1, keepdims=True) + 1e-06)
    return center * inverse, inverse


def norm_back(d_normal, normal, inverse):
    return inverse * (
        d_normal
        - jnp.mean(d_normal, axis=-1, keepdims=True)
        - normal * jnp.mean(d_normal * normal, axis=-1, keepdims=True)
    )


def middle_kernel(
    chunk,
    turn_ref,
    tok,
    mixed_keep,
    mixed_recv,
    lse_keep,
    w_out_own,
    w_out_oth,
    w_up_own,
    w_up_oth,
    w_down_own,
    w_down_oth,
    gain,
    shift,
    grad_out,
    out,
    d_resid,
    payload,
    active_own,
    active_oth,
    d_up_own,
    d_up_oth,
    d_ffn_out,
    normed_out,
    small,
    slope,
):
    seqs, half, width = out.shape
    rows = seqs * half
    heads = mixed_keep.shape[2] // HEAD_DIM
    keep = mixed_keep[...].reshape(rows, -1)
    recv = mixed_recv[:, :half, :].reshape(rows, -1)
    attn = dot_nn(keep, w_out_own[...]) + dot_nn(recv, w_out_oth[...])
    resid_one = tok[:, :half, :].reshape(rows, width).astype(full) + attn
    normal_one, inverse_one = norm_of(resid_one)
    gain_one, gain_two = gain[0:1, :], gain[1:2, :]
    normed = normal_one * gain_one + shift[0:1, :]
    normed_low = normed.astype(low)
    normed_out[...] = normed_low
    units = w_up_own.shape[0]
    sides = ((w_up_own, w_down_own, active_own, d_up_own), (w_up_oth, w_down_oth, active_oth, d_up_oth))
    ffn = jnp.zeros((rows, width), full)
    for which, (w_up, w_down, active_ref, _) in enumerate(sides):
        for start in range(0, units, chunk):
            part = slice(start, start + chunk)
            upward = dot_nt(normed_low, w_up[part, :])
            spread = 0.5 * (1.0 + lax.erf(upward * 0.7071067811865476))
            active = (upward * spread).astype(low)
            slope[:, which * units + start : which * units + start + chunk] = (
                spread + upward * (jnp.exp(upward * upward * -0.5) * 0.3989422804014327)
            )
            active_ref[:, part] = active
            ffn = ffn + dot_nn(active, w_down[part, :])
    normal_two, inverse_two = norm_of(normed + ffn)
    out[...] = (normal_two * gain_two + shift[1:2, :]).astype(low).reshape(seqs, half, width)
    grad = grad_out[...].reshape(rows, width).astype(full)
    small[1:2, :] = jnp.sum(grad * normal_two, axis=0, keepdims=True)
    small[3:4, :] = jnp.sum(grad, axis=0, keepdims=True)
    d_resid_two = norm_back(grad * gain_two, normal_two, inverse_two)
    d_ffn = d_resid_two.astype(low)
    d_ffn_out[...] = d_ffn
    d_normed = d_resid_two
    for which, (w_up, w_down, _, d_up_ref) in enumerate(sides):
        for start in range(0, units, chunk):
            part = slice(start, start + chunk)
            d_active = dot_nt(d_ffn, w_down[part, :])
            d_up = (d_active * slope[:, which * units + start : which * units + start + chunk]).astype(low)
            d_up_ref[:, part] = d_up
            d_normed = d_normed + dot_nn(d_up, w_up[part, :])
    small[0:1, :] = jnp.sum(d_normed * normal_one, axis=0, keepdims=True)
    small[2:3, :] = jnp.sum(d_normed, axis=0, keepdims=True)
    small[4:8, :] = jnp.zeros((4, width), full)
    d_resid_one = norm_back(d_normed * gain_one, normal_one, inverse_one)
    d_resid[...] = d_resid_one.reshape(seqs, half, width)
    d_attn = d_resid_one.astype(low)
    payload[:, :half, :] = d_attn.reshape(seqs, half, width)
    column_of = lax.broadcasted_iota(jnp.int32, (8, heads * HEAD_DIM), 1) // HEAD_DIM
    chosen = jnp.where(column_of == lax.broadcasted_iota(jnp.int32, (8, heads * HEAD_DIM), 0), 1.0, 0.0)
    deltas = []
    for mixed, w_out in ((keep, w_out_own), (recv, w_out_oth)):
        d_mixed = dot_nt(d_attn, w_out[...]).astype(low).astype(full)
        deltas.append(
            lax.dot_general(
                chosen,
                d_mixed * mixed.astype(full),
                (((1,), (1,)), ((), ())),
                precision=lax.Precision.HIGHEST,
                preferred_element_type=full,
            )
        )
    row_of = lax.broadcasted_iota(jnp.int32, (STAT_ROWS, half), 0)
    pairs = heads // 2
    for seq in range(seqs):
        for head in range(heads):
            lse_high, lse_low = two_parts(lse_keep[seq, head : head + 1, :half])
            tile = slice((head % pairs) * LANES, (head % pairs + 1) * LANES)
            row = half + 2 * (head // pairs)
            parts = [lse_high.astype(full), lse_low.astype(full)]
            for which in range(2):
                piece = deltas[which][head : head + 1, seq * half : (seq + 1) * half]
                if which == 1:
                    parts.append(mixed_recv[seq, row : row + 1, tile].astype(full))
                    parts.append(mixed_recv[seq, row + 1 : row + 2, tile].astype(full))
                parts.extend(part.astype(full) for part in two_parts(piece))
            stat = jnp.zeros((STAT_ROWS, half), full)
            for index, part in enumerate(parts):
                stat = jnp.where(row_of == index, part, stat)
            payload[seq, half:, head * LANES : (head + 1) * LANES] = stat.astype(low)


def slot_order(count):
    if count == 1:
        return [0]
    inner = slot_order(count // 2)
    return [2 * slot + 1 for slot in inner] + [2 * slot for slot in inner]


def reversed_bits(value, bits):
    return sum(((value >> bit) & 1) << (bits - 1 - bit) for bit in range(bits))


def lasting(microseconds):
    return pl.CostEstimate(flops=int(microseconds * 1.15e+09), transcendentals=0, bytes_accessed=0)


def far(value):
    return pltpu.with_memory_space_constraint(value, pltpu.HBM)


def whole(shape):
    return pl.BlockSpec(shape, lambda *_: (0,) * len(shape), pipeline_mode=pl.Buffered(1))


def kernel_params(megabytes):
    return pltpu.CompilerParams(vmem_limit_bytes=megabytes << 20)


def on_device(
    ctx_size,
    dp_size,
    tokens,
    segment_ids,
    w_qkv,
    w_out,
    w_up,
    w_down,
    norm_gain,
    norm_bias,
    grad_out,
):
    seqs, span, width = tokens.shape
    half = span // 2
    local_width = w_out.shape[0]
    heads = local_width // HEAD_DIM
    units_local = w_up.shape[0]
    rows = seqs * half
    long_half = half + STAT_ROWS
    ctx_bits = ctx_size.bit_length() - 1
    turn = lax.axis_index("tensor")
    place = lax.axis_index("ctx")
    row_place = lax.axis_index("dp")
    turn_array = turn.reshape(1)

    def room(megabytes):
        return kernel_params(megabytes if ctx_size <= 4 else 60)

    def swap(value):
        return lax.ppermute(value, "tensor", [(0, 1), (1, 0)])

    def hop(value, stage):
        moves = []
        for spot in range(ctx_size):
            for core in range(2):
                bit = stage if core == 0 else ctx_bits - 1 - stage
                moves.append((spot * 2 + core, (spot ^ (1 << bit)) * 2 + core))
        return lax.ppermute(value, ("ctx", "tensor"), moves)

    def tie(*values):
        return lax.optimization_barrier(values)

    def gather_near(own):
        own = own[:, None]
        return [hop(own, stage) for stage in range(min(ctx_bits, 2))]

    def gather_far(own, near_groups):
        groups = list(near_groups)
        if ctx_bits >= 2:
            groups.append(hop(groups[0], 1))
        for stage in range(2, ctx_bits):
            groups.append(hop(jnp.concatenate([own[:, None]] + groups, axis=1), stage))
        return groups

    def half_of(value, which):
        return lax.dynamic_slice_in_dim(value, which * half, half, 1)

    def with_ids(which):
        ids = half_of(segment_ids, which).astype(low)
        row = jnp.pad(ids[:, None, :], ((0, 0), (0, STAT_ROWS - 1), (0, width - half)))
        return jnp.concatenate([half_of(tokens, which), row], axis=1)

    def units_of(groups):
        direct, swapped = groups[: len(groups) // 2], groups[len(groups) // 2 :]
        if ctx_size == 4:
            return [(direct[0], swapped[1]), (direct[1], swapped[0]), (direct[2], swapped[2])]
        mirror = [reversed_bits(slot, ctx_bits) - 1 for slot in range(1, ctx_size)]
        first, second = jnp.concatenate(direct, axis=1), jnp.concatenate(swapped, axis=1)
        return [(first, jnp.stack([second[:, slot] for slot in mirror], axis=1))]

    block_width = 3 * local_width + LANES
    part_spec = pl.BlockSpec((1, 1, long_half, width), lambda g, s: (s, g, 0, 0))

    def project(part_a, part_b):
        count = part_a.shape[1]
        return pl.pallas_call(
            project_kernel,
            grid=(count, seqs),
            in_specs=[whole(w_qkv.shape), part_spec, part_spec],
            out_specs=pl.BlockSpec((1, 1, span, block_width), lambda g, s: (s, g, 0, 0)),
            out_shape=jax.ShapeDtypeStruct((seqs, count, span, block_width), low),
            compiler_params=room(16),
            cost_estimate=lasting(2),
            name="project",
        )(w_qkv, part_a, part_b)

    tok_a, tok_b = with_ids(turn), with_ids(1 - turn)
    tok_near = gather_near(tok_a)
    w_out_oth, w_up_oth, w_down_oth = swap(w_out), swap(w_up), swap(w_down)
    own = project(tok_a[:, None], tok_b[:, None])

    def seq_spec(shape):
        return pl.BlockSpec((1,) + shape, lambda s, *_: (s,) + (0,) * len(shape))

    def unit_specs(chosen):
        return [
            pl.BlockSpec(
                (1,) + value.shape[1:],
                lambda s, *_: (s, 0, 0, 0),
                pipeline_mode=pl.Buffered(2 if value.shape[1] == 1 else 1),
            )
            for value in chosen
        ]

    head_square = pltpu.VMEM((heads, span, span), full)
    head_square_low = pltpu.VMEM((heads, span, span), low)
    q_scratch = pltpu.VMEM((heads, span, 2 * LANES), low)
    head_rows = pltpu.VMEM((heads, span, LANES), low)

    def attend(chosen, state, finish):
        begin = state is None
        state_shapes = [((local_width, span), full), ((16, span), full)]
        shapes = (
            [((half, local_width), low), ((long_half, local_width), low), ((8, span), full)]
            if finish
            else state_shapes
        )
        state = [] if begin else list(state)
        return pl.pallas_call(
            functools.partial(attend_kernel, [value.shape[1] for value in chosen], heads, begin, finish),
            grid=(seqs,),
            in_specs=unit_specs([own] + chosen) + [seq_spec(value.shape[1:]) for value in state],
            out_specs=[seq_spec(shape) for shape, _ in shapes],
            out_shape=[
                (pltpu.HBM if finish else jax.ShapeDtypeStruct)((seqs,) + shape, kind) for shape, kind in shapes
            ],
            scratch_shapes=[
                q_scratch,
                head_square,
                head_square_low,
                pltpu.VMEM((16, span), full),
                pltpu.VMEM((local_width, span), full),
            ],
            compiler_params=room(14),
            cost_estimate=lasting(3),
            name="attend",
        )(own, *chosen, *state)

    state = attend([], None, False)
    *tok_near, first_state = tie(*tok_near, state[0])
    state = (first_state, state[1])
    tok_groups = gather_far(tok_a, tok_near)
    if ctx_size == 4:
        swapped = [swap(group) for group in tok_groups[:2]]
        near_units = [project(tok_groups[0], swapped[1]), project(tok_groups[1], swapped[0])]
        state = attend(near_units, state, False)
        last, first_state = tie(tok_groups[2], state[0])
        far_units = [project(last, swap(last))]
        units = near_units + far_units
        mixed_keep, mixed_send, lse = attend(far_units, (first_state, state[1]), True)
    else:
        units = [project(*pair) for pair in units_of(tok_groups + [swap(group) for group in tok_groups])]
        mixed_keep, mixed_send, lse = attend(units, state, True)
    mixed_recv = swap(mixed_send)

    middle_in = [
        tok_a,
        mixed_keep,
        mixed_recv,
        lse,
        w_out,
        w_out_oth,
        w_up,
        w_up_oth,
        w_down,
        w_down_oth,
        norm_gain,
        norm_bias,
    ]
    middle_shapes = [
        ((seqs, half, width), low),
        ((seqs, half, width), full),
        ((seqs, long_half, width), low),
        ((rows, units_local), low),
        ((rows, units_local), low),
        ((rows, units_local), low),
        ((rows, units_local), low),
        ((rows, width), low),
        ((rows, width), low),
        ((8, width), full),
    ]
    (
        out_half,
        d_resid,
        payload,
        active_own,
        active_oth,
        d_up_own,
        d_up_oth,
        d_ffn,
        normed_low,
        small,
    ) = pl.pallas_call(
        functools.partial(middle_kernel, min(512, units_local)),
        grid_spec=pltpu.PrefetchScalarGridSpec(
            num_scalar_prefetch=1,
            grid=(1,),
            in_specs=[whole(value.shape) for value in middle_in]
            + [pl.BlockSpec((seqs, half, width), lambda s, turn_ref: (0, turn_ref[0], 0))],
            out_specs=[whole(shape) for shape, _ in middle_shapes],
            scratch_shapes=[pltpu.VMEM((rows, 2 * units_local), full)],
        ),
        out_shape=[
            (jax.ShapeDtypeStruct if number == 2 else pltpu.HBM)(shape, kind)
            for number, (shape, kind) in enumerate(middle_shapes)
        ],
        compiler_params=room(36),
        cost_estimate=lasting(16),
        name="middle",
    )(turn_array, *middle_in, grad_out)

    order = slot_order(ctx_size)
    mirrored = [reversed_bits(slot, ctx_bits) for slot in order]
    owners = place ^ jnp.where(turn == 0, jnp.array(order, jnp.int32), jnp.array(mirrored, jnp.int32))
    quarter = width // ctx_size
    stages = [ctx_size >> (stage + 1) for stage in range(ctx_bits)] + [1]
    turned_kind = low if quarter % 16 == 0 else full
    chunk = min(512, units_local)

    def slot_scratch(count):
        return [pltpu.VMEM((width, count), turned_kind), pltpu.VMEM((ctx_size * padded(quarter), count), low)]

    def pair_grad(left_a, left_b, right_a, right_b, name):
        right_spec = pl.BlockSpec((rows, chunk), lambda n, *_: (0, n))
        return pl.pallas_call(
            pair_grad_kernel,
            grid_spec=pltpu.PrefetchScalarGridSpec(
                num_scalar_prefetch=1,
                grid=(units_local // chunk,),
                in_specs=[whole(left_a.shape), whole(left_b.shape), right_spec, right_spec],
                out_specs=[pl.BlockSpec((count, quarter, chunk), lambda n, *_: (0, 0, n)) for count in stages],
                scratch_shapes=slot_scratch(2 * rows),
            ),
            out_shape=[pltpu.HBM((count, quarter, units_local), low) for count in stages],
            compiler_params=room(16),
            cost_estimate=lasting(5.5),
            name=name,
        )(owners, *map(far, (left_a, left_b, right_a, right_b)))

    parity = row_place & 1

    def add_up(values):
        return sum(value.astype(full) for value in values)

    def send_stage(parts, gots, stage):
        count, start = parts[stage].shape[0], 0
        values = [parts[stage]]
        for got in gots:
            start = got.shape[0] - sum(part.shape[0] for part in parts[stage:])
            values.append(got[start : start + count])
        return add_up(values).astype(low)

    def own_half(parts, gots, which):
        values = [parts[-1]] + gots
        split = parts[-1].shape[1] // 2
        return add_up(
            [
                lax.dynamic_slice(value, (value.shape[0] - 1, which * split, 0), (1, split, value.shape[2]))
                for value in values
            ]
        )[0]

    class Blocks:
        def __init__(self, parts):
            self.parts, self.gots, self.stage, self.sent = list(parts), [], 0, None
            self.dp_stage, self.got = 0, None

        @property
        def arrived(self):
            return self.gots[-1] if self.dp_stage == 0 else self.got

        @arrived.setter
        def arrived(self, value):
            if self.dp_stage == 0:
                self.gots[-1] = value
            else:
                self.got = value

        def ready(self):
            if self.stage < ctx_bits:
                self.sent = send_stage(self.parts, self.gots, self.stage) if self.stage else self.parts[0]
            elif self.dp_stage == 0:
                self.sent = own_half(self.parts, self.gots, 1 - parity).astype(low)
            else:
                mine = own_half(self.parts, self.gots, parity) if self.dp_stage == 1 else self.sent.astype(full)
                self.sent = (mine + self.got.astype(full)).astype(low)

        def send(self):
            if self.stage < ctx_bits:
                self.gots.append(hop(self.sent, self.stage))
                self.stage += 1
                return
            last = self.dp_stage == dp_size.bit_length() - 1
            bit = 0 if last else self.dp_stage
            moves = [(spot, spot ^ (1 << bit)) for spot in range(dp_size)]
            self.got = lax.ppermute(self.sent, "dp", moves)
            self.dp_stage += 1

        def advance(self, *after):
            if self.gots:
                self.arrived = tie(self.arrived, *after)[0]
            elif after:
                self.parts[0] = tie(self.parts[0], *after)[0]
            self.ready()
            self.send()
            return self.sent

        def total(self):
            while self.dp_stage < dp_size.bit_length():
                self.advance()
            mine, other = self.sent, self.got
            return jnp.where(
                parity == 0, jnp.concatenate([mine, other], axis=0), jnp.concatenate([other, mine], axis=0)
            ).astype(full)

    grad_near = gather_near(payload)
    payload_b = swap(payload)
    d_ffn_b, active_b = swap(d_ffn), swap(active_oth)
    normed_b, d_up_b = swap(normed_low), swap(d_up_oth)
    down = Blocks(pair_grad(d_ffn, d_ffn_b, active_own, active_b, "grad_down"))
    latest = down.advance()
    normed_low, latest = tie(normed_low, latest)
    up = Blocks(pair_grad(normed_low, normed_b, d_up_own, d_up_b, "grad_up"))
    *grad_near, up.parts[0] = tie(*grad_near, up.parts[0])
    latest = up.advance()
    own_back, latest = tie(own, latest)
    grad_far = gather_far(payload, grad_near)
    grad_groups = grad_far + [swap(group) for group in grad_far]

    sum_shape = pltpu.HBM((seqs, span, local_width), full)
    row_shape = pltpu.HBM((seqs, span, local_width), low)
    grad_spec = seq_spec((long_half, width))
    span_spec = seq_spec((span, local_width))
    counts = [value.shape[1] for value in units]
    d_query, dk_sum, dv_sum = pl.pallas_call(
        functools.partial(query_grad_kernel, counts, heads),
        grid=(seqs,),
        in_specs=unit_specs([own]) + [grad_spec, grad_spec, whole(w_out.shape)] + unit_specs(units),
        out_specs=[span_spec] * 3,
        out_shape=[row_shape, sum_shape, sum_shape],
        scratch_shapes=[
            q_scratch,
            head_rows,
            pltpu.VMEM((16, span), full),
            head_square,
            head_square_low,
            head_square_low,
            pltpu.VMEM((local_width, span), full),
        ],
        compiler_params=room(20),
        cost_estimate=lasting(11),
        name="query_grad",
    )(own_back, payload, payload_b, far(w_out), *units)

    def sequence_grad(kernel, values, lefts, extra, columns, name):
        return Blocks(
            pl.pallas_call(
                kernel,
                grid_spec=pltpu.PrefetchScalarGridSpec(
                    num_scalar_prefetch=1,
                    grid=(1,),
                    in_specs=[whole(value.shape) for value in values],
                    out_specs=[whole((count, extra + quarter, columns)) for count in stages],
                    scratch_shapes=slot_scratch(seqs * span) * lefts,
                ),
                out_shape=[pltpu.HBM((count, extra + quarter, columns), low) for count in stages],
                compiler_params=room(20),
                cost_estimate=lasting(5.5),
                name=name,
            )(owners, *map(far, values))
        )

    small_rows = (small[:4] + swap(small)[:4]).reshape(4, ctx_size, quarter).transpose(1, 0, 2)
    small_rows = jnp.pad(small_rows, ((0, 0), (0, STAT_ROWS - 4), (0, local_width - quarter)))
    latest = down.advance(d_query)
    d_query, latest = tie(d_query, latest)
    query_out = sequence_grad(
        query_out_grad_kernel,
        (tok_a, tok_b, d_query, payload, payload_b, mixed_keep, mixed_send, small_rows),
        2,
        STAT_ROWS,
        2 * local_width,
        "query_out_grad",
    )
    latest = query_out.advance()
    latest = down.advance(latest)
    d_query, latest = tie(d_query, latest)
    grad_units = units_of(grad_groups)
    grad_a, grad_b = [pair[0] for pair in grad_units], [pair[1] for pair in grad_units]
    d_kv, d_input = pl.pallas_call(
        functools.partial(key_grad_kernel, counts, heads),
        grid_spec=pltpu.PrefetchScalarGridSpec(
            num_scalar_prefetch=1,
            grid=(seqs,),
            in_specs=unit_specs([own])
            + [span_spec] * 3
            + [whole(w_out.shape), whole(w_qkv.shape)]
            + unit_specs(units + grad_a + grad_b),
            out_specs=[seq_spec((span, 2 * local_width)), seq_spec((span, width))],
            scratch_shapes=[
                pltpu.VMEM((heads // 2, span, 2 * LANES), low),
                head_rows,
                head_rows,
                head_square,
                head_square_low,
                head_square_low,
                pltpu.VMEM((span, local_width), full),
                pltpu.VMEM((span, local_width), full),
            ],
        ),
        out_shape=[
            jax.ShapeDtypeStruct((seqs, span, 2 * local_width), low),
            jax.ShapeDtypeStruct((seqs, span, width), low),
        ],
        compiler_params=room(26),
        cost_estimate=lasting(12.5),
        name="key_grad",
    )(turn_array, own, *map(far, (d_query, dk_sum, dv_sum, w_out, w_qkv, *units)), *grad_a, *grad_b)

    latest = up.advance(d_kv)
    latest = down.advance(latest)
    latest = query_out.advance(latest)
    d_kv, latest = tie(d_kv, latest)
    key_value = sequence_grad(key_value_grad_kernel, (tok_a, tok_b, d_kv), 1, 0, 2 * local_width, "key_value_grad")
    latest = key_value.advance()
    out_half, d_resid, d_input, latest = tie(out_half, d_resid, d_input, latest)
    swapped = [swap(out_half), swap(d_resid), swap(d_input)]
    for blocks in (up, down, key_value, query_out):
        latest = blocks.advance(latest)

    def both_halves(mine, other):
        return jnp.where(
            turn == 0, jnp.concatenate([mine, other], axis=1), jnp.concatenate([other, mine], axis=1)
        )

    *swapped, latest = tie(*swapped, latest)
    outputs = both_halves(out_half, swapped[0])
    grad_tokens = d_input.astype(full) + swapped[2].astype(full) + both_halves(d_resid, swapped[1])
    outputs, grad_tokens, latest = tie(outputs, grad_tokens, latest)
    for blocks in (up, key_value, query_out, up, key_value, query_out, key_value):
        latest = blocks.advance(latest)
    down_total, up_total = down.total(), up.total()
    query_out_total, key_value_total = query_out.total(), key_value.total()
    small_total = query_out_total[:4, local_width : local_width + quarter]
    query_out_total = query_out_total[STAT_ROWS:]
    return (
        outputs,
        grad_tokens,
        jnp.stack(
            [query_out_total[:, :local_width], key_value_total[:, :local_width], key_value_total[:, local_width:]]
        ),
        query_out_total[:, local_width:].T,
        up_total.T,
        down_total.T,
        small_total[0:2],
        small_total[2:4],
    )


def solution(mesh):
    return jax.shard_map(
        functools.partial(on_device, mesh.shape["ctx"], mesh.shape["dp"]),
        mesh=mesh,
        in_specs=(
            P("dp", "ctx", None),
            P("dp", "ctx"),
            P(None, None, "tensor"),
            P("tensor", None),
            P("tensor", None),
            P("tensor", None),
            P(),
            P(),
            P("dp", "ctx", None),
        ),
        out_specs=(
            P("dp", "ctx", None),
            P("dp", "ctx", None),
            P(None, "ctx", "tensor"),
            P("tensor", "ctx"),
            P("tensor", "ctx"),
            P("tensor", "ctx"),
            P(None, "ctx"),
            P(None, "ctx"),
        ),
        check_vma=False,
    )
```

profile of v0, /device:TPU:0, one launch (start us, length us, event | category | flops | bytes accessed | tf_op | source)
XLA Modules:
  0.0 213.0 jit_solution(4769988361296746319)
XLA Ops:
  2.8 3.0 %collective-permute-start = (bf16[3,1,144,768]{3,2,0,1:T(8,128)(2,1)S(1)}, bf16[3,1,144,768]{3,2,0,1:T(8,128)(2,1)S(1)}, u32[]{:S(2)}, u32[]{:S(2)}) collective-permute-start(bf16[3,1,144,768]{3,2,0,1:T(8,128)(2,1)S(1)} %get-tuple-element.154), channel_id=1, source_target_pairs={{0,2},{1,5},{2,0},{3,7},{4,6},{5,1},{6,4},{7,3},{8,10},{9,13},{10,... | collective-permute-start | bytes 1990664 | tf_op jit(solution)/shard_map/ppermute | solution.py:587
  10.7 2.4 %attend.3 = (f32[3,384,256]{2,1,0:T(8,128)S(1)}, f32[3,16,256]{2,1,0:T(8,128)S(1)}) custom-call(bf16[3,1,256,1280]{3,2,1,0:T(8,128)(2,1)S(1)} %project.4.refs_0_), custom_call_target="tpu_custom_call" | custom-call | flops 3449999872 | tf_op jit(solution)/shard_map/attend/pallas_call | solution.py:668
  13.1 7.9 %collective-permute-done = bf16[3,1,144,768]{3,2,0,1:T(8,128)(2,1)S(1)} collective-permute-done((bf16[3,1,144,768]{3,2,0,1:T(8,128)(2,1)S(1)}, bf16[3,1,144,768]{3,2,0,1:T(8,128)(2,1)S(1)}, u32[]{:S(2)}, u32[]{:S(2)}) %collective-permute-start) | collective-permute-done | bytes 663584 | tf_op jit(solution)/shard_map/ppermute | solution.py:587
  28.4 3.9 %attend.4 = (f32[3,384,256]{2,1,0:T(8,128)S(1)}, f32[3,16,256]{2,1,0:T(8,128)S(1)}) custom-call(bf16[3,1,256,1280]{3,2,1,0:T(8,128)(2,1)S(1)} %project.4.refs_0_, bf16[3,1,256,1280]{3,2,1,0:T(8,128)(2,1)S(1)} %project.5.refs_1_.refs_4_.refs_6_, bf16[3,1,256,1280]{3,2,1,0:T(8,128)(2,1)S(1)} %project.6.refs_2_.refs_5_.refs_7_, ...), custom_call_target="tpu_custom_call" | custom-call | flops 3449999872 | tf_op jit(solution)/shard_map/attend/pallas_call | solution.py:668
  43.1 14.7 %middle.1 = (bf16[3,128,768]{2,1,0:T(8,128)(2,1)}, f32[3,128,768]{2,1,0:T(8,128)}, bf16[3,144,768]{2,1,0:T(8,128)(2,1)S(1)}, bf16[384,1536]{1,0:T(8,128)(2,1)}, ...) custom-call(s32[1]{0:T(128)} %bitcast.turn_ref, ...), custom_call_target="tpu_custom_call" | custom-call | flops 18400000000 | tf_op jit(solution)/shard_map/middle/pallas_call | solution.py:742
  58.8 3.8 %collective-permute-start.10 = (bf16[3,1,144,768]{3,2,1,0:T(8,128)(2,1)S(1)}, bf16[3,1,144,768]{3,2,1,0:T(8,128)(2,1)S(1)}, u32[]{:S(2)}, u32[]{:S(2)}) collective-permute-start(bf16[3,1,144,768]{3,2,1,0:T(8,128)(2,1)S(1)} %bitcast.60), channel_id=1, source_target_pairs={{0,2},{1,5},{2,0},{3,7},{4,6},{5,1},{6,4},{7,3},{8,10},{9,13},{10,... | collective-permute-start | bytes 1990664 | tf_op jit(solution)/shard_map/ppermute | solution.py:587
  62.7 2.5 %collective-permute-start.11 = (bf16[3,1,144,768]{3,2,1,0:T(8,128)(2,1)S(1)}, bf16[3,1,144,768]{3,2,1,0:T(8,128)(2,1)S(1)}, u32[]{:S(2)}, u32[]{:S(2)}) collective-permute-start(bf16[3,1,144,768]{3,2,1,0:T(8,128)(2,1)S(1)} %bitcast.61), channel_id=1, source_target_pairs={{0,4},{1,3},{2,6},{3,1},{4,0},{5,7},{6,2},{7,5},{8,12},{9,11},{10,... | collective-permute-start | bytes 1990664 | tf_op jit(solution)/shard_map/ppermute | solution.py:587
  67.8 6.7 %grad_down.1 = (bf16[2,192,1536]{2,1,0:T(8,128)(2,1)}, bf16[1,192,1536]{2,1,0:T(8,128)(2,1)}, bf16[1,192,1536]{2,1,0:T(8,128)(2,1)}) custom-call(s32[4]{0:T(128)S(1)} %fusion.19.owners, bf16[384,768]{1,0:T(8,128)(2,1)} %get-tuple-element.93.left_a, bf16[384,768]{1,0:T(8,128)(2,1)} %copy-done.33, bf16[384,1536]{1,0:T(8,128)(2,1)} %get-tuple-element.94.right_a, ...), custom_call_target="tpu_custom_call" | custom-call | flops 6325000192 | tf_op jit(solution)/shard_map/grad_down/pallas_call | solution.py:774
  75.3 6.8 %grad_up.1 = (bf16[2,192,1536]{2,1,0:T(8,128)(2,1)}, bf16[1,192,1536]{2,1,0:T(8,128)(2,1)}, bf16[1,192,1536]{2,1,0:T(8,128)(2,1)}) custom-call(s32[4]{0:T(128)S(1)} %fusion.19.owners, bf16[384,768]{1,0:T(8,128)(2,1)} %get-tuple-element.97.left_a, bf16[384,768]{1,0:T(8,128)(2,1)} %copy-done.34, bf16[384,1536]{1,0:T(8,128)(2,1)} %get-tuple-element.98.right_a, ...), custom_call_target="tpu_custom_call" | custom-call | flops 6325000192 | tf_op jit(solution)/shard_map/grad_up/pallas_call | solution.py:774
  85.0 9.8 %query_grad.1 = (bf16[3,256,384]{2,1,0:T(8,128)(2,1)}, f32[3,256,384]{2,1,0:T(8,128)}, f32[3,256,384]{2,1,0:T(8,128)}) custom-call(bf16[3,1,256,1280]{3,2,1,0:T(8,128)(2,1)S(1)} %copy-done.11, bf16[3,144,768]{2,1,0:T(8,128)(2,1)S(1)} %get-tuple-element.91.refs_1_.d_attn_a, bf16[3,144,768]{2,1,0:T(8,128)(2,1)S(1)} %collective-permute-done.16.refs_2_.d_attn_b, ...), custom_call_target="tpu_custom_call" | custom-call | flops 12650000384 | tf_op jit(solution)/shard_map/query_grad/pallas_call | solution.py:884
  94.7 5.3 %collective-permute-done.20.refs_11_ = bf16[3,1,144,768]{3,2,1,0:T(8,128)(2,1)S(1)} collective-permute-done((bf16[3,1,144,768]{3,2,1,0:T(8,128)(2,1)S(1)}, bf16[3,1,144,768]{3,2,1,0:T(8,128)(2,1)S(1)}, u32[]{:S(2)}, u32[]{:S(2)}) %collective-permute-start.20) | collective-permute-done | bytes 663584 | tf_op jit(solution)/shard_map/ppermute | solution.py:587
  102.2 6.4 %query_out_grad.1 = (bf16[2,208,768]{2,1,0:T(8,128)(2,1)}, bf16[1,208,768]{2,1,0:T(8,128)(2,1)}, bf16[1,208,768]{2,1,0:T(8,128)(2,1)}) custom-call(s32[4]{0:T(128)S(1)} %fusion.19.owners, bf16[3,144,768]{2,1,0:T(8,128)(2,1)} %copy-done, bf16[3,144,768]{2,1,0:T(8,128)(2,1)} %get-tuple-element.152.tok_b, ...), custom_call_target="tpu_custom_call" | custom-call | flops 6325000192 | tf_op jit(solution)/shard_map/query_out_grad/pallas_call | solution.py:906
  108.7 7.8 %collective-permute-done.18 = bf16[1,192,1536]{2,1,0:T(8,128)(2,1)S(1)} collective-permute-done((bf16[1,192,1536]{2,1,0:T(8,128)(2,1)S(1)}, bf16[1,192,1536]{2,1,0:T(8,128)(2,1)S(1)}, u32[]{:S(2)}, u32[]{:S(2)}) %collective-permute-start.18) | collective-permute-done | bytes 589856 | tf_op jit(solution)/shard_map/ppermute | solution.py:587
  119.1 11.0 %key_grad.1 = (bf16[3,256,768]{2,1,0:T(8,128)(2,1)S(1)}, bf16[3,256,768]{2,1,0:T(8,128)(2,1)S(1)}) custom-call(s32[1]{0:T(128)} %bitcast.turn_ref, bf16[3,1,256,1280]{3,2,1,0:T(8,128)(2,1)S(1)} %copy-done.11, bf16[3,256,384]{2,1,0:T(8,128)(2,1)} %get-tuple-element.111.d_query.refs_1_, f32[3,256,384]{2,1,0:T(8,128)} %get-tuple-element.112.refs_2_, ...), custom_call_target="tpu_custom_call" | custom-call | flops 14375000064 | tf_op jit(solution)/shard_map/key_grad/pallas_call | solution.py:939
  130.2 3.4 %collective-permute-start.33 = (bf16[1,192,1536]{2,1,0:T(8,128)(2,1)S(1)}, bf16[1,192,1536]{2,1,0:T(8,128)(2,1)S(1)}, u32[]{:S(2)}, u32[]{:S(2)}) collective-permute-start(bf16[1,192,1536]{2,1,0:T(8,128)(2,1)S(1)} %add_convert_fusion), channel_id=1, source_target_pairs={{0,4},{1,3},{2,6},{3,1},{4,0},{5,7},{6,2},{7,5},{8,12},{9,11},{10,... | collective-permute-start | bytes 1769480 | tf_op jit(solution)/shard_map/ppermute | solution.py:587
  135.0 2.6 %collective-permute-start.32 = (bf16[96,1536]{1,0:T(8,128)(2,1)S(1)}, bf16[96,1536]{1,0:T(8,128)(2,1)S(1)}, u32[]{:S(2)}, u32[]{:S(2)}) collective-permute-start(bf16[96,1536]{1,0:T(8,128)(2,1)S(1)} %fusion.6), channel_id=1, source_target_pairs={{0,16},{8,24},{16,0},{24,8},{1,17},{9,25},{17,1},{25,9},{2,18},{10... | collective-permute-start | bytes 884744 | tf_op jit(solution)/shard_map/ppermute | solution.py:845
  137.5 5.1 %key_value_grad.1 = (bf16[2,192,768]{2,1,0:T(8,128)(2,1)}, bf16[1,192,768]{2,1,0:T(8,128)(2,1)}, bf16[1,192,768]{2,1,0:T(8,128)(2,1)}) custom-call(s32[4]{0:T(128)S(1)} %fusion.19.owners, bf16[3,144,768]{2,1,0:T(8,128)(2,1)} %copy-done, bf16[3,144,768]{2,1,0:T(8,128)(2,1)} %get-tuple-element.152.tok_b, bf16[3,256,768]{2,1,0:T(8,128)(2,1)} %copy-done.19), custom_call_target="tpu_custom_call" | custom-call | flops 6325000192 | tf_op jit(solution)/shard_map/key_value_grad/pallas_call | solution.py:906
  144.2 5.4 %collective-permute-done.32 = bf16[96,1536]{1,0:T(8,128)(2,1)S(1)} collective-permute-done((bf16[96,1536]{1,0:T(8,128)(2,1)S(1)}, bf16[96,1536]{1,0:T(8,128)(2,1)S(1)}, u32[]{:S(2)}, u32[]{:S(2)}) %collective-permute-start.32) | collective-permute-done | bytes 294944 | tf_op jit(solution)/shard_map/ppermute | solution.py:845
  149.8 8.8 %collective-permute-done.36 = bf16[96,1536]{1,0:T(8,128)(2,1)S(1)} collective-permute-done((bf16[96,1536]{1,0:T(8,128)(2,1)S(1)}, bf16[96,1536]{1,0:T(8,128)(2,1)S(1)}, u32[]{:S(2)}, u32[]{:S(2)}) %collective-permute-start.36) | collective-permute-done | bytes 294944 | tf_op jit(solution)/shard_map/ppermute | solution.py:845
  159.9 8.3 %collective-permute-done.44 = bf16[96,1536]{1,0:T(8,128)(2,1)S(1)} collective-permute-done((bf16[96,1536]{1,0:T(8,128)(2,1)S(1)}, bf16[96,1536]{1,0:T(8,128)(2,1)S(1)}, u32[]{:S(2)}, u32[]{:S(2)}) %collective-permute-start.44) | collective-permute-done | bytes 294944 | tf_op jit(solution)/shard_map/ppermute | solution.py:845
  169.8 5.5 %collective-permute-done.34 = bf16[104,768]{1,0:T(8,128)(2,1)S(1)} collective-permute-done((bf16[104,768]{1,0:T(8,128)(2,1)S(1)}, bf16[104,768]{1,0:T(8,128)(2,1)S(1)}, u32[]{:S(2)}, u32[]{:S(2)}) %collective-permute-start.34) | collective-permute-done | bytes 159776 | tf_op jit(solution)/shard_map/ppermute | solution.py:845
  175.7 9.8 %collective-permute-done.39 = bf16[96,1536]{1,0:T(8,128)(2,1)S(1)} collective-permute-done((bf16[96,1536]{1,0:T(8,128)(2,1)S(1)}, bf16[96,1536]{1,0:T(8,128)(2,1)S(1)}, u32[]{:S(2)}, u32[]{:S(2)}) %collective-permute-start.39) | collective-permute-done | bytes 294944 | tf_op jit(solution)/shard_map/ppermute | solution.py:845
  187.5 6.1 %collective-permute-done.37 = bf16[104,768]{1,0:T(8,128)(2,1)S(1)} collective-permute-done((bf16[104,768]{1,0:T(8,128)(2,1)S(1)}, bf16[104,768]{1,0:T(8,128)(2,1)S(1)}, u32[]{:S(2)}, u32[]{:S(2)}) %collective-permute-start.37) | collective-permute-done | bytes 159776 | tf_op jit(solution)/shard_map/ppermute | solution.py:845
  193.7 9.1 %collective-permute-done.41 = bf16[96,768]{1,0:T(8,128)(2,1)S(1)} collective-permute-done((bf16[96,768]{1,0:T(8,128)(2,1)S(1)}, bf16[96,768]{1,0:T(8,128)(2,1)S(1)}, u32[]{:S(2)}, u32[]{:S(2)}) %collective-permute-start.41) | collective-permute-done | bytes 147488 | tf_op jit(solution)/shard_map/ppermute | solution.py:845
  (187 shorter events, 55.5 us)
Async XLA Ops:
  2.8 18.2 %collective-permute-start = (bf16[3,1,144,768]{3,2,0,1:T(8,128)(2,1)S(1)}, bf16[3,1,144,768]{3,2,0,1:T(8,128)(2,1)S(1)}, u32[]{:S(2)}, u32[]{:S(2)}) collective-permute-start(bf16[3,1,144,768]{3,2,0,1:T(8,128)(2,1)S(1)} %get-tuple-element.154), channel_id=1, source_target_pairs={{0,2},{1,5},{2,0},{3,7},{4,6},{5,1},{6,4},{7,3},{8,10},{9,13},{10,... | collective-permute-start | bytes 1990664 | tf_op jit(solution)/shard_map/ppermute | solution.py:587
  5.8 15.2 %collective-permute-start.1 = (bf16[3,1,144,768]{3,2,0,1:T(8,128)(2,1)S(1)}, bf16[3,1,144,768]{3,2,0,1:T(8,128)(2,1)S(1)}, u32[]{:S(2)}, u32[]{:S(2)}) collective-permute-start(bf16[3,1,144,768]{3,2,0,1:T(8,128)(2,1)S(1)} %get-tuple-element.154), channel_id=1, source_target_pairs={{0,4},{1,3},{2,6},{3,1},{4,0},{5,7},{6,2},{7,5},{8,12},{9,11},{10,... | collective-permute-start | bytes 1990664 | tf_op jit(solution)/shard_map/ppermute | solution.py:587
  21.6 19.8 %collective-permute-start.8 = (bf16[1536,768]{1,0:T(8,128)(2,1)S(1)}, bf16[1536,768]{1,0:T(8,128)(2,1)S(1)}, u32[]{:S(2)}, u32[]{:S(2)}) collective-permute-start(bf16[1536,768]{1,0:T(8,128)(2,1)S(1)} %copy-done.1), channel_id=1, source_target_pairs={{0,1},{1,0},{2,3},{3,2},{4,5},{5,4},{6,7},{7,6},{8,9},{9,8},{10,11... | collective-permute-start | bytes 7077896 | tf_op jit(solution)/shard_map/ppermute | solution.py:579
  21.9 19.4 %collective-permute-start.9 = (bf16[1536,768]{1,0:T(8,128)(2,1)S(1)}, bf16[1536,768]{1,0:T(8,128)(2,1)S(1)}, u32[]{:S(2)}, u32[]{:S(2)}) collective-permute-start(bf16[1536,768]{1,0:T(8,128)(2,1)S(1)} %copy-done.2), channel_id=1, source_target_pairs={{0,1},{1,0},{2,3},{3,2},{4,5},{5,4},{6,7},{7,6},{8,9},{9,8},{10,11... | collective-permute-start | bytes 7077896 | tf_op jit(solution)/shard_map/ppermute | solution.py:579
  58.3 16.9 %collective-permute-start.15 = (bf16[384,1536]{1,0:T(8,128)(2,1)}, bf16[384,1536]{1,0:T(8,128)(2,1)}, u32[]{:S(2)}, u32[]{:S(2)}) collective-permute-start(bf16[384,1536]{1,0:T(8,128)(2,1)} %get-tuple-element.99), channel_id=1, source_target_pairs={{0,1},{1,0},{2,3},{3,2},{4,5},{5,4},{6,7},{7,6},{8,9},{9,8},{10,11... | collective-permute-start | bytes 3538952 | tf_op jit(solution)/shard_map/ppermute | solution.py:579
  58.8 23.3 %collective-permute-start.10 = (bf16[3,1,144,768]{3,2,1,0:T(8,128)(2,1)S(1)}, bf16[3,1,144,768]{3,2,1,0:T(8,128)(2,1)S(1)}, u32[]{:S(2)}, u32[]{:S(2)}) collective-permute-start(bf16[3,1,144,768]{3,2,1,0:T(8,128)(2,1)S(1)} %bitcast.60), channel_id=1, source_target_pairs={{0,2},{1,5},{2,0},{3,7},{4,6},{5,1},{6,4},{7,3},{8,10},{9,13},{10,... | collective-permute-start | bytes 1990664 | tf_op jit(solution)/shard_map/ppermute | solution.py:587
  62.7 19.4 %collective-permute-start.11 = (bf16[3,1,144,768]{3,2,1,0:T(8,128)(2,1)S(1)}, bf16[3,1,144,768]{3,2,1,0:T(8,128)(2,1)S(1)}, u32[]{:S(2)}, u32[]{:S(2)}) collective-permute-start(bf16[3,1,144,768]{3,2,1,0:T(8,128)(2,1)S(1)} %bitcast.61), channel_id=1, source_target_pairs={{0,4},{1,3},{2,6},{3,1},{4,0},{5,7},{6,2},{7,5},{8,12},{9,11},{10,... | collective-permute-start | bytes 1990664 | tf_op jit(solution)/shard_map/ppermute | solution.py:587
  66.7 18.2 %collective-permute-start.16 = (bf16[3,144,768]{2,1,0:T(8,128)(2,1)S(1)}, bf16[3,144,768]{2,1,0:T(8,128)(2,1)S(1)}, u32[]{:S(2)}, u32[]{:S(2)}) collective-permute-start(bf16[3,144,768]{2,1,0:T(8,128)(2,1)S(1)} %get-tuple-element.91.refs_1_.d_attn_a), channel_id=1, source_target_pairs={{0,1},{1,0},{2,3},{3,2},{4,5},{5,4},{6,7},{7,6},{8,9},{9,8},{10,11... | collective-permute-start | bytes 1990664 | tf_op jit(solution)/shard_map/ppermute | solution.py:579
  74.5 25.5 %collective-permute-start.17 = (bf16[2,192,1536]{2,1,0:T(8,128)(2,1)}, bf16[2,192,1536]{2,1,0:T(8,128)(2,1)S(1)}, u32[]{:S(2)}, u32[]{:S(2)}) collective-permute-start(bf16[2,192,1536]{2,1,0:T(8,128)(2,1)} %get-tuple-element.96), channel_id=1, source_target_pairs={{0,2},{1,5},{2,0},{3,7},{4,6},{5,1},{6,4},{7,3},{8,10},{9,13},{10,... | collective-permute-start | bytes 3538952 | tf_op jit(solution)/shard_map/ppermute | solution.py:587
  82.1 17.9 %collective-permute-start.20 = (bf16[3,1,144,768]{3,2,1,0:T(8,128)(2,1)S(1)}, bf16[3,1,144,768]{3,2,1,0:T(8,128)(2,1)S(1)}, u32[]{:S(2)}, u32[]{:S(2)}) collective-permute-start(bf16[3,1,144,768]{3,2,1,0:T(8,128)(2,1)S(1)} %collective-permute-done.10.refs_9_), channel_id=1, source_target_pairs={{0,4},{1,3},{2,6},{3,1},{4,0},{5,7},{6,2},{7,5},{8,12},{9,11},{10,... | collective-permute-start | bytes 1990664 | tf_op jit(solution)/shard_map/ppermute | solution.py:587
  84.2 34.9 %collective-permute-start.22 = (bf16[3,1,144,768]{3,2,1,0:T(8,128)(2,1)S(1)}, bf16[3,1,144,768]{3,2,1,0:T(8,128)(2,1)S(1)}, u32[]{:S(2)}, u32[]{:S(2)}) collective-permute-start(bf16[3,1,144,768]{3,2,1,0:T(8,128)(2,1)S(1)} %collective-permute-done.10.refs_9_), channel_id=1, source_target_pairs={{0,1},{1,0},{2,3},{3,2},{4,5},{5,4},{6,7},{7,6},{8,9},{9,8},{10,11... | collective-permute-start | bytes 1990664 | tf_op jit(solution)/shard_map/ppermute | solution.py:579
  84.2 45.9 %collective-permute-start.26 = (bf16[2,192,1536]{2,1,0:T(8,128)(2,1)}, bf16[2,192,1536]{2,1,0:T(8,128)(2,1)S(1)}, u32[]{:S(2)}, u32[]{:S(2)}) collective-permute-start(bf16[2,192,1536]{2,1,0:T(8,128)(2,1)} %get-tuple-element.101), channel_id=1, source_target_pairs={{0,2},{1,5},{2,0},{3,7},{4,6},{5,1},{6,4},{7,3},{8,10},{9,13},{10,... | collective-permute-start | bytes 3538952 | tf_op jit(solution)/shard_map/ppermute | solution.py:587
  84.9 33.0 %collective-permute-start.21 = (bf16[3,1,144,768]{3,2,1,0:T(8,128)(2,1)S(1)}, bf16[3,1,144,768]{3,2,1,0:T(8,128)(2,1)S(1)}, u32[]{:S(2)}, u32[]{:S(2)}) collective-permute-start(bf16[3,1,144,768]{3,2,1,0:T(8,128)(2,1)S(1)} %collective-permute-done.11.refs_10_), channel_id=1, source_target_pairs={{0,1},{1,0},{2,3},{3,2},{4,5},{5,4},{6,7},{7,6},{8,9},{9,8},{10,11... | collective-permute-start | bytes 1990664 | tf_op jit(solution)/shard_map/ppermute | solution.py:579
  100.0 19.0 %collective-permute-start.23 = (bf16[3,1,144,768]{3,2,1,0:T(8,128)(2,1)S(1)}, bf16[3,1,144,768]{3,2,1,0:T(8,128)(2,1)S(1)}, u32[]{:S(2)}, u32[]{:S(2)}) collective-permute-start(bf16[3,1,144,768]{3,2,1,0:T(8,128)(2,1)S(1)} %collective-permute-done.20.refs_11_), channel_id=1, source_target_pairs={{0,1},{1,0},{2,3},{3,2},{4,5},{5,4},{6,7},{7,6},{8,9},{9,8},{10,11... | collective-permute-start | bytes 1990664 | tf_op jit(solution)/shard_map/ppermute | solution.py:579
  100.2 16.3 %collective-permute-start.18 = (bf16[1,192,1536]{2,1,0:T(8,128)(2,1)S(1)}, bf16[1,192,1536]{2,1,0:T(8,128)(2,1)S(1)}, u32[]{:S(2)}, u32[]{:S(2)}) collective-permute-start(bf16[1,192,1536]{2,1,0:T(8,128)(2,1)S(1)} %add_convert_fusion.1), channel_id=1, source_target_pairs={{0,4},{1,3},{2,6},{3,1},{4,0},{5,7},{6,2},{7,5},{8,12},{9,11},{10,... | collective-permute-start | bytes 1769480 | tf_op jit(solution)/shard_map/ppermute | solution.py:587
  116.5 17.3 %collective-permute-start.24 = (bf16[2,208,768]{2,1,0:T(8,128)(2,1)}, bf16[2,208,768]{2,1,0:T(8,128)(2,1)S(1)}, u32[]{:S(2)}, u32[]{:S(2)}) collective-permute-start(bf16[2,208,768]{2,1,0:T(8,128)(2,1)} %get-tuple-element.109), channel_id=1, source_target_pairs={{0,2},{1,5},{2,0},{3,7},{4,6},{5,1},{6,4},{7,3},{8,10},{9,13},{10,... | collective-permute-start | bytes 1916936 | tf_op jit(solution)/shard_map/ppermute | solution.py:587
  118.0 15.7 %collective-permute-start.25 = (bf16[96,1536]{1,0:T(8,128)(2,1)S(1)}, bf16[96,1536]{1,0:T(8,128)(2,1)S(1)}, u32[]{:S(2)}, u32[]{:S(2)}) collective-permute-start(bf16[96,1536]{1,0:T(8,128)(2,1)S(1)} %fusion.9), channel_id=1, source_target_pairs={{0,8},{8,0},{16,24},{24,16},{1,9},{9,1},{17,25},{25,17},{2,10},{10... | collective-permute-start | bytes 884744 | tf_op jit(solution)/shard_map/ppermute | solution.py:845
  133.9 25.3 %collective-permute-start.30 = (bf16[1,208,768]{2,1,0:T(8,128)(2,1)S(1)}, bf16[1,208,768]{2,1,0:T(8,128)(2,1)S(1)}, u32[]{:S(2)}, u32[]{:S(2)}) collective-permute-start(bf16[1,208,768]{2,1,0:T(8,128)(2,1)S(1)} %add_convert_fusion.2), channel_id=1, source_target_pairs={{0,4},{1,3},{2,6},{3,1},{4,0},{5,7},{6,2},{7,5},{8,12},{9,11},{10,... | collective-permute-start | bytes 958472 | tf_op jit(solution)/shard_map/ppermute | solution.py:587
  142.6 16.1 %collective-permute-start.31 = (bf16[2,192,768]{2,1,0:T(8,128)(2,1)}, bf16[2,192,768]{2,1,0:T(8,128)(2,1)S(1)}, u32[]{:S(2)}, u32[]{:S(2)}) collective-permute-start(bf16[2,192,768]{2,1,0:T(8,128)(2,1)} %get-tuple-element.124), channel_id=1, source_target_pairs={{0,2},{1,5},{2,0},{3,7},{4,6},{5,1},{6,4},{7,3},{8,10},{9,13},{10,... | collective-permute-start | bytes 1769480 | tf_op jit(solution)/shard_map/ppermute | solution.py:587
  143.6 62.4 %collective-permute-start.27 = (bf16[3,128,768]{2,1,0:T(8,128)(2,1)S(1)}, bf16[3,128,768]{2,1,0:T(8,128)(2,1)S(1)}, u32[]{:S(2)}, u32[]{:S(2)}) collective-permute-start(bf16[3,128,768]{2,1,0:T(8,128)(2,1)S(1)} %copy-done.22), channel_id=1, source_target_pairs={{0,1},{1,0},{2,3},{3,2},{4,5},{5,4},{6,7},{7,6},{8,9},{9,8},{10,11... | collective-permute-start | bytes 1769480 | tf_op jit(solution)/shard_map/ppermute | solution.py:579
  143.6 62.4 %collective-permute-start.28 = (f32[3,128,768]{2,1,0:T(8,128)S(1)}, f32[3,128,768]{2,1,0:T(8,128)S(1)}, u32[]{:S(2)}, u32[]{:S(2)}) collective-permute-start(f32[3,128,768]{2,1,0:T(8,128)S(1)} %copy-done.21), channel_id=1, source_target_pairs={{0,1},{1,0},{2,3},{3,2},{4,5},{5,4},{6,7},{7,6},{8,9},{9,8},{10,11... | collective-permute-start | bytes 3538952 | tf_op jit(solution)/shard_map/ppermute | solution.py:579
  158.6 47.4 %collective-permute-start.29 = (bf16[3,256,768]{2,1,0:T(8,128)(2,1)S(1)}, bf16[3,256,768]{2,1,0:T(8,128)(2,1)S(1)}, u32[]{:S(2)}, u32[]{:S(2)}) collective-permute-start(bf16[3,256,768]{2,1,0:T(8,128)(2,1)S(1)} %get-tuple-element.127), channel_id=1, source_target_pairs={{0,1},{1,0},{2,3},{3,2},{4,5},{5,4},{6,7},{7,6},{8,9},{9,8},{10,11... | collective-permute-start | bytes 3538952 | tf_op jit(solution)/shard_map/ppermute | solution.py:579
  169.7 15.7 %collective-permute-start.39 = (bf16[96,1536]{1,0:T(8,128)(2,1)S(1)}, bf16[96,1536]{1,0:T(8,128)(2,1)S(1)}, u32[]{:S(2)}, u32[]{:S(2)}) collective-permute-start(bf16[96,1536]{1,0:T(8,128)(2,1)S(1)} %fusion.5), channel_id=1, source_target_pairs={{0,16},{8,24},{16,0},{24,8},{1,17},{9,25},{17,1},{25,9},{2,18},{10... | collective-permute-start | bytes 884744 | tf_op jit(solution)/shard_map/ppermute | solution.py:845
  185.5 17.3 %collective-permute-start.43 = (bf16[96,1536]{1,0:T(8,128)(2,1)S(1)}, bf16[96,1536]{1,0:T(8,128)(2,1)S(1)}, u32[]{:S(2)}, u32[]{:S(2)}) collective-permute-start(bf16[96,1536]{1,0:T(8,128)(2,1)S(1)} %add_convert_fusion.3), channel_id=1, source_target_pairs={{0,8},{8,0},{16,24},{24,16},{1,9},{9,1},{17,25},{25,17},{2,10},{10... | collective-permute-start | bytes 884744 | tf_op jit(solution)/shard_map/ppermute | solution.py:845
  (56 other events, 510.7 us)
where the time goes:
time: 214 us; the launch traced here: 213 us
  waiting for transfers between devices  78.8 us (37%)
  Pallas kernels  78.3 us (37%)
  starting transfers between devices  38.6 us (18%)
  other arithmetic  10.7 us (5%)
  local copies, waits for them, and re-layouts  5.34 us (2%)
    ppermute x12, waiting for transfers between devices, send(): self.got = lax.ppermute(self.sent, 'dp', moves)  54.1 us
    ppermute x14, starting transfers between devices, hop(): return lax.ppermute(value, ('ctx', 'tensor'), moves)  25.4 us
    ppermute x14, waiting for transfers between devices, hop(): return lax.ppermute(value, ('ctx', 'tensor'), moves)  21.5 us
    pallas_call x1, Pallas kernels, on_device(): pl.pallas_call(functools.partial(middle_kernel, min(512, units_local)), g...  14.7 us
    pallas_call x2, Pallas kernels, pair_grad(): pl.pallas_call(pair_grad_kernel, grid_spec=pltpu.PrefetchScalarGridSpec(n...  13.5 us
    pallas_call x2, Pallas kernels, sequence_grad(): pl.pallas_call(kernel, grid_spec=pltpu.PrefetchScalarGridSpec(num_scalar_...  11.5 us
    pallas_call x1, Pallas kernels, on_device(): pl.pallas_call(functools.partial(key_grad_kernel, counts, heads), grid_sp...  11 us
    pallas_call x1, Pallas kernels, on_device(): pl.pallas_call(functools.partial(query_grad_kernel, counts, heads), grid=...  9.78 us
  transfers between devices with their start and end apart: 45, of which 15 were waited for; matrix products, arithmetic and copies ran while one was open for 5% of the time, Pallas kernels for 30%

commit v1 on v0

--- a/solution.py
+++ b/solution.py
@@ -874,7 +874,7 @@
     latest = up.advance()
     own_back, latest = tie(own, latest)
     grad_far = gather_far(payload, grad_near)
-    grad_groups = grad_far + [swap(group) for group in grad_far]
+    crossed = [swap(group) for group in grad_far[:-1]]
 
     sum_shape = pltpu.HBM((seqs, span, local_width), full)
     row_shape = pltpu.HBM((seqs, span, local_width), low)
@@ -931,10 +931,12 @@
         2 * local_width,
         "query_out_grad",
     )
+    grad_far[-1], query_out.parts[1] = tie(grad_far[-1], query_out.parts[1])
+    crossed.append(swap(grad_far[-1]))
     latest = query_out.advance()
     latest = down.advance(latest)
     d_query, latest = tie(d_query, latest)
-    grad_units = units_of(grad_groups)
+    grad_units = units_of(grad_far + crossed)
     grad_a, grad_b = [pair[0] for pair in grad_units], [pair[1] for pair in grad_units]
     d_kv, d_input = pl.pallas_call(
         functools.partial(key_grad_kernel, counts, heads),
@@ -964,7 +966,7 @@
         compiler_params=room(26),
         cost_estimate=lasting(12.5),
         name="key_grad",
-    )(turn_array, own, *map(far, (d_query, dk_sum, dv_sum, w_out, w_qkv, *units)), *grad_a, *grad_b)
+    )(turn_array, own, *map(far, (d_query, dk_sum, dv_sum, w_out, w_qkv, *units, *grad_a, *grad_b)))
 
     latest = up.advance(d_kv)
     latest = down.advance(latest)

time: 214 us -> 207 us (0.967)
  waiting for transfers between devices: 78.8 us -> 64.2 us
  starting transfers between devices: 38.6 us -> 45.2 us
  Pallas kernels: 78.3 us -> 76 us
    ppermute x12, waiting for transfers between devices: 54.1 us -> 42.3 us  [send(): self.got = lax.ppermute(self.sent, 'dp', moves)]
    ppermute x12, starting transfers between devices: 8.67 us -> 18.8 us  [send(): self.got = lax.ppermute(self.sent, 'dp', moves)]
    ppermute x14, waiting for transfers between devices: 21.5 us -> 16.5 us  [hop(): return lax.ppermute(value, ('ctx', 'tensor'), moves)]
    ppermute x14, starting transfers between devices: 25.4 us -> 21.8 us  [hop(): return lax.ppermute(value, ('ctx', 'tensor'), moves)]
    ppermute x19, waiting for transfers between devices: 3.16 us -> 5.4 us  [swap(): return lax.ppermute(value, 'tensor', [(0, 1), (1, 0)])]
  transfers between devices with their start and end apart: 45 -> 45, of which waited for: 15 -> 17; matrix products, arithmetic and copies ran while one was open for 5% -> 6% of each run, Pallas kernels for 30% -> 30%
where the time goes in v1:
time: 207 us; the launch traced here: 206 us
  Pallas kernels  76 us (37%)
  waiting for transfers between devices  64.2 us (31%)
  starting transfers between devices  45.2 us (22%)
  other arithmetic  12.8 us (6%)
  local copies, waits for them, and re-layouts  6.31 us (3%)
    ppermute x12, waiting for transfers between devices, send(): self.got = lax.ppermute(self.sent, 'dp', moves)  42.3 us
    ppermute x14, starting transfers between devices, hop(): return lax.ppermute(value, ('ctx', 'tensor'), moves)  21.8 us
    ppermute x12, starting transfers between devices, send(): self.got = lax.ppermute(self.sent, 'dp', moves)  18.8 us
    ppermute x14, waiting for transfers between devices, hop(): return lax.ppermute(value, ('ctx', 'tensor'), moves)  16.5 us
    pallas_call x1, Pallas kernels, on_device(): pl.pallas_call(functools.partial(middle_kernel, min(512, units_local)), g...  14.7 us
    pallas_call x2, Pallas kernels, pair_grad(): pl.pallas_call(pair_grad_kernel, grid_spec=pltpu.PrefetchScalarGridSpec(n...  13.4 us
    pallas_call x2, Pallas kernels, sequence_grad(): pl.pallas_call(kernel, grid_spec=pltpu.PrefetchScalarGridSpec(num_scalar_...  11.2 us
    pallas_call x1, Pallas kernels, on_device(): pl.pallas_call(functools.partial(key_grad_kernel, counts, heads), grid_sp...  10.4 us
  transfers between devices with their start and end apart: 45, of which 17 were waited for; matrix products, arithmetic and copies ran while one was open for 6% of the time, Pallas kernels for 30%

profile of v1, /device:TPU:0, one launch (start us, length us, event | category | flops | bytes accessed | tf_op | source)
XLA Modules:
  0.0 205.8 jit_solution(9601187826101821329)
XLA Ops:
  2.8 3.0 %collective-permute-start = (bf16[3,1,144,768]{3,2,0,1:T(8,128)(2,1)S(1)}, bf16[3,1,144,768]{3,2,0,1:T(8,128)(2,1)S(1)}, u32[]{:S(2)}, u32[]{:S(2)}) collective-permute-start(bf16[3,1,144,768]{3,2,0,1:T(8,128)(2,1)S(1)} %get-tuple-element.158), channel_id=1, source_target_pairs={{0,2},{1,5},{2,0},{3,7},{4,6},{5,1},{6,4},{7,3},{8,10},{9,13},{10,... | collective-permute-start | bytes 1990664 | tf_op jit(solution)/shard_map/ppermute | solution.py:587
  10.7 2.4 %attend.3 = (f32[3,384,256]{2,1,0:T(8,128)S(1)}, f32[3,16,256]{2,1,0:T(8,128)S(1)}) custom-call(bf16[3,1,256,1280]{3,2,1,0:T(8,128)(2,1)S(1)} %project.4.refs_0_), custom_call_target="tpu_custom_call" | custom-call | flops 3449999872 | tf_op jit(solution)/shard_map/attend/pallas_call | solution.py:668
  13.1 7.9 %collective-permute-done = bf16[3,1,144,768]{3,2,0,1:T(8,128)(2,1)S(1)} collective-permute-done((bf16[3,1,144,768]{3,2,0,1:T(8,128)(2,1)S(1)}, bf16[3,1,144,768]{3,2,0,1:T(8,128)(2,1)S(1)}, u32[]{:S(2)}, u32[]{:S(2)}) %collective-permute-start) | collective-permute-done | bytes 663584 | tf_op jit(solution)/shard_map/ppermute | solution.py:587
  28.4 3.1 %attend.4 = (f32[3,384,256]{2,1,0:T(8,128)S(1)}, f32[3,16,256]{2,1,0:T(8,128)S(1)}) custom-call(bf16[3,1,256,1280]{3,2,1,0:T(8,128)(2,1)S(1)} %project.4.refs_0_, bf16[3,1,256,1280]{3,2,1,0:T(8,128)(2,1)S(1)} %project.5.refs_1_.refs_4_.refs_6_, bf16[3,1,256,1280]{3,2,1,0:T(8,128)(2,1)S(1)} %project.6.refs_2_.refs_5_.refs_7_, ...), custom_call_target="tpu_custom_call" | custom-call | flops 3449999872 | tf_op jit(solution)/shard_map/attend/pallas_call | solution.py:668
  43.0 14.7 %middle.1 = (bf16[3,128,768]{2,1,0:T(8,128)(2,1)}, f32[3,128,768]{2,1,0:T(8,128)}, bf16[3,144,768]{2,1,0:T(8,128)(2,1)S(1)}, bf16[384,1536]{1,0:T(8,128)(2,1)}, ...) custom-call(s32[1]{0:T(128)} %bitcast.turn_ref, ...), custom_call_target="tpu_custom_call" | custom-call | flops 18400000000 | tf_op jit(solution)/shard_map/middle/pallas_call | solution.py:742
  58.8 2.5 %collective-permute-start.10 = (bf16[3,1,144,768]{3,2,1,0:T(8,128)(2,1)S(1)}, bf16[3,1,144,768]{3,2,1,0:T(8,128)(2,1)}, u32[]{:S(2)}, u32[]{:S(2)}) collective-permute-start(bf16[3,1,144,768]{3,2,1,0:T(8,128)(2,1)S(1)} %bitcast.60), channel_id=1, source_target_pairs={{0,2},{1,5},{2,0},{3,7},{4,6},{5,1},{6,4},{7,3},{8,10},{9,13},{10,... | collective-permute-start | bytes 1990664 | tf_op jit(solution)/shard_map/ppermute | solution.py:587
  67.3 6.6 %grad_down.1 = (bf16[2,192,1536]{2,1,0:T(8,128)(2,1)}, bf16[1,192,1536]{2,1,0:T(8,128)(2,1)}, bf16[1,192,1536]{2,1,0:T(8,128)(2,1)}) custom-call(s32[4]{0:T(128)S(1)} %fusion.19.owners, bf16[384,768]{1,0:T(8,128)(2,1)} %get-tuple-element.95.left_a, bf16[384,768]{1,0:T(8,128)(2,1)} %copy-done.35, bf16[384,1536]{1,0:T(8,128)(2,1)} %get-tuple-element.96.right_a, ...), custom_call_target="tpu_custom_call" | custom-call | flops 6325000192 | tf_op jit(solution)/shard_map/grad_down/pallas_call | solution.py:774
  76.6 6.7 %grad_up.1 = (bf16[2,192,1536]{2,1,0:T(8,128)(2,1)}, bf16[1,192,1536]{2,1,0:T(8,128)(2,1)}, bf16[1,192,1536]{2,1,0:T(8,128)(2,1)}) custom-call(s32[4]{0:T(128)S(1)} %fusion.19.owners, bf16[384,768]{1,0:T(8,128)(2,1)} %get-tuple-element.99.left_a, bf16[384,768]{1,0:T(8,128)(2,1)} %copy-done.36, bf16[384,1536]{1,0:T(8,128)(2,1)} %get-tuple-element.100.right_a, ...), custom_call_target="tpu_custom_call" | custom-call | flops 6325000192 | tf_op jit(solution)/shard_map/grad_up/pallas_call | solution.py:774
  85.3 9.2 %query_grad.1 = (bf16[3,256,384]{2,1,0:T(8,128)(2,1)}, f32[3,256,384]{2,1,0:T(8,128)}, f32[3,256,384]{2,1,0:T(8,128)}) custom-call(bf16[3,1,256,1280]{3,2,1,0:T(8,128)(2,1)S(1)} %copy-done.11, bf16[3,144,768]{2,1,0:T(8,128)(2,1)S(1)} %get-tuple-element.93.refs_1_.d_attn_a, bf16[3,144,768]{2,1,0:T(8,128)(2,1)S(1)} %collective-permute-done.16.refs_2_.d_attn_b, ...), custom_call_target="tpu_custom_call" | custom-call | flops 12650000384 | tf_op jit(solution)/shard_map/query_grad/pallas_call | solution.py:884
  96.6 6.4 %query_out_grad.1 = (bf16[2,208,768]{2,1,0:T(8,128)(2,1)}, bf16[1,208,768]{2,1,0:T(8,128)(2,1)}, bf16[1,208,768]{2,1,0:T(8,128)(2,1)}) custom-call(s32[4]{0:T(128)S(1)} %fusion.19.owners, bf16[3,144,768]{2,1,0:T(8,128)(2,1)} %copy-done, bf16[3,144,768]{2,1,0:T(8,128)(2,1)} %get-tuple-element.156.tok_b, ...), custom_call_target="tpu_custom_call" | custom-call | flops 6325000192 | tf_op jit(solution)/shard_map/query_out_grad/pallas_call | solution.py:906
  103.1 2.4 %collective-permute-start.26 = (bf16[2,192,1536]{2,1,0:T(8,128)(2,1)}, bf16[2,192,1536]{2,1,0:T(8,128)(2,1)S(1)}, u32[]{:S(2)}, u32[]{:S(2)}) collective-permute-start(bf16[2,192,1536]{2,1,0:T(8,128)(2,1)} %get-tuple-element.103), channel_id=1, source_target_pairs={{0,2},{1,5},{2,0},{3,7},{4,6},{5,1},{6,4},{7,3},{8,10},{9,13},{10,... | collective-permute-start | bytes 3538952 | tf_op jit(solution)/shard_map/ppermute | solution.py:587
  108.3 5.1 %collective-permute-start.25 = (bf16[96,1536]{1,0:T(8,128)(2,1)S(1)}, bf16[96,1536]{1,0:T(8,128)(2,1)S(1)}, u32[]{:S(2)}, u32[]{:S(2)}) collective-permute-start(bf16[96,1536]{1,0:T(8,128)(2,1)S(1)} %fusion.9), channel_id=1, source_target_pairs={{0,8},{8,0},{16,24},{24,16},{1,9},{9,1},{17,25},{25,17},{2,10},{10... | collective-permute-start | bytes 884744 | tf_op jit(solution)/shard_map/ppermute | solution.py:845
  113.4 10.4 %key_grad.1 = (bf16[3,256,768]{2,1,0:T(8,128)(2,1)S(1)}, bf16[3,256,768]{2,1,0:T(8,128)(2,1)S(1)}) custom-call(s32[1]{0:T(128)} %bitcast.turn_ref, bf16[3,1,256,1280]{3,2,1,0:T(8,128)(2,1)S(1)} %copy-done.11, bf16[3,256,384]{2,1,0:T(8,128)(2,1)} %get-tuple-element.113.d_query.refs_1_, f32[3,256,384]{2,1,0:T(8,128)} %get-tuple-element.114.refs_2_, ...), custom_call_target="tpu_custom_call" | custom-call | flops 14375000064 | tf_op jit(solution)/shard_map/key_grad/pallas_call | solution.py:941
  126.3 2.5 %collective-permute-done.24 = bf16[2,208,768]{2,1,0:T(8,128)(2,1)S(1)} collective-permute-done((bf16[2,208,768]{2,1,0:T(8,128)(2,1)}, bf16[2,208,768]{2,1,0:T(8,128)(2,1)S(1)}, u32[]{:S(2)}, u32[]{:S(2)}) %collective-permute-start.24) | collective-permute-done | bytes 639008 | tf_op jit(solution)/shard_map/ppermute | solution.py:587
  129.0 7.4 %collective-permute-start.32 = (bf16[96,1536]{1,0:T(8,128)(2,1)S(1)}, bf16[96,1536]{1,0:T(8,128)(2,1)S(1)}, u32[]{:S(2)}, u32[]{:S(2)}) collective-permute-start(bf16[96,1536]{1,0:T(8,128)(2,1)S(1)} %fusion.6), channel_id=1, source_target_pairs={{0,16},{8,24},{16,0},{24,8},{1,17},{9,25},{17,1},{25,9},{2,18},{10... | collective-permute-start | bytes 884744 | tf_op jit(solution)/shard_map/ppermute | solution.py:845
  136.4 4.8 %key_value_grad.1 = (bf16[2,192,768]{2,1,0:T(8,128)(2,1)}, bf16[1,192,768]{2,1,0:T(8,128)(2,1)}, bf16[1,192,768]{2,1,0:T(8,128)(2,1)}) custom-call(s32[4]{0:T(128)S(1)} %fusion.19.owners, bf16[3,144,768]{2,1,0:T(8,128)(2,1)} %copy-done, bf16[3,144,768]{2,1,0:T(8,128)(2,1)} %get-tuple-element.156.tok_b, bf16[3,256,768]{2,1,0:T(8,128)(2,1)} %copy-done.19), custom_call_target="tpu_custom_call" | custom-call | flops 6325000192 | tf_op jit(solution)/shard_map/key_value_grad/pallas_call | solution.py:906
  143.0 5.2 %collective-permute-done.32 = bf16[96,1536]{1,0:T(8,128)(2,1)S(1)} collective-permute-done((bf16[96,1536]{1,0:T(8,128)(2,1)S(1)}, bf16[96,1536]{1,0:T(8,128)(2,1)S(1)}, u32[]{:S(2)}, u32[]{:S(2)}) %collective-permute-start.32) | collective-permute-done | bytes 294944 | tf_op jit(solution)/shard_map/ppermute | solution.py:845
  148.3 3.0 %collective-permute-done.31 = bf16[2,192,768]{2,1,0:T(8,128)(2,1)S(1)} collective-permute-done((bf16[2,192,768]{2,1,0:T(8,128)(2,1)}, bf16[2,192,768]{2,1,0:T(8,128)(2,1)S(1)}, u32[]{:S(2)}, u32[]{:S(2)}) %collective-permute-start.31) | collective-permute-done | bytes 589856 | tf_op jit(solution)/shard_map/ppermute | solution.py:587
  153.6 7.4 %collective-permute-done.36 = bf16[96,1536]{1,0:T(8,128)(2,1)S(1)} collective-permute-done((bf16[96,1536]{1,0:T(8,128)(2,1)S(1)}, bf16[96,1536]{1,0:T(8,128)(2,1)S(1)}, u32[]{:S(2)}, u32[]{:S(2)}) %collective-permute-start.36) | collective-permute-done | bytes 294944 | tf_op jit(solution)/shard_map/ppermute | solution.py:845
  161.8 3.0 %collective-permute-done.44 = bf16[96,1536]{1,0:T(8,128)(2,1)S(1)} collective-permute-done((bf16[96,1536]{1,0:T(8,128)(2,1)S(1)}, bf16[96,1536]{1,0:T(8,128)(2,1)S(1)}, u32[]{:S(2)}, u32[]{:S(2)}) %collective-permute-start.44) | collective-permute-done | bytes 294944 | tf_op jit(solution)/shard_map/ppermute | solution.py:845
  168.3 6.0 %collective-permute-done.34 = bf16[104,768]{1,0:T(8,128)(2,1)S(1)} collective-permute-done((bf16[104,768]{1,0:T(8,128)(2,1)S(1)}, bf16[104,768]{1,0:T(8,128)(2,1)S(1)}, u32[]{:S(2)}, u32[]{:S(2)}) %collective-permute-start.34) | collective-permute-done | bytes 159776 | tf_op jit(solution)/shard_map/ppermute | solution.py:845
  174.4 5.8 %collective-permute-done.39 = bf16[96,1536]{1,0:T(8,128)(2,1)S(1)} collective-permute-done((bf16[96,1536]{1,0:T(8,128)(2,1)S(1)}, bf16[96,1536]{1,0:T(8,128)(2,1)S(1)}, u32[]{:S(2)}, u32[]{:S(2)}) %collective-permute-start.39) | collective-permute-done | bytes 294944 | tf_op jit(solution)/shard_map/ppermute | solution.py:845
  183.4 7.1 %collective-permute-done.37 = bf16[104,768]{1,0:T(8,128)(2,1)S(1)} collective-permute-done((bf16[104,768]{1,0:T(8,128)(2,1)S(1)}, bf16[104,768]{1,0:T(8,128)(2,1)S(1)}, u32[]{:S(2)}, u32[]{:S(2)}) %collective-permute-start.37) | collective-permute-done | bytes 159776 | tf_op jit(solution)/shard_map/ppermute | solution.py:845
  190.6 6.1 %collective-permute-done.41 = bf16[96,768]{1,0:T(8,128)(2,1)S(1)} collective-permute-done((bf16[96,768]{1,0:T(8,128)(2,1)S(1)}, bf16[96,768]{1,0:T(8,128)(2,1)S(1)}, u32[]{:S(2)}, u32[]{:S(2)}) %collective-permute-start.41) | collective-permute-done | bytes 147488 | tf_op jit(solution)/shard_map/ppermute | solution.py:845
  (191 shorter events, 65.5 us)
Async XLA Ops:
  2.8 18.2 %collective-permute-start = (bf16[3,1,144,768]{3,2,0,1:T(8,128)(2,1)S(1)}, bf16[3,1,144,768]{3,2,0,1:T(8,128)(2,1)S(1)}, u32[]{:S(2)}, u32[]{:S(2)}) collective-permute-start(bf16[3,1,144,768]{3,2,0,1:T(8,128)(2,1)S(1)} %get-tuple-element.158), channel_id=1, source_target_pairs={{0,2},{1,5},{2,0},{3,7},{4,6},{5,1},{6,4},{7,3},{8,10},{9,13},{10,... | collective-permute-start | bytes 1990664 | tf_op jit(solution)/shard_map/ppermute | solution.py:587
  5.8 15.2 %collective-permute-start.1 = (bf16[3,1,144,768]{3,2,0,1:T(8,128)(2,1)S(1)}, bf16[3,1,144,768]{3,2,0,1:T(8,128)(2,1)S(1)}, u32[]{:S(2)}, u32[]{:S(2)}) collective-permute-start(bf16[3,1,144,768]{3,2,0,1:T(8,128)(2,1)S(1)} %get-tuple-element.158), channel_id=1, source_target_pairs={{0,4},{1,3},{2,6},{3,1},{4,0},{5,7},{6,2},{7,5},{8,12},{9,11},{10,... | collective-permute-start | bytes 1990664 | tf_op jit(solution)/shard_map/ppermute | solution.py:587
  21.6 19.7 %collective-permute-start.8 = (bf16[1536,768]{1,0:T(8,128)(2,1)S(1)}, bf16[1536,768]{1,0:T(8,128)(2,1)S(1)}, u32[]{:S(2)}, u32[]{:S(2)}) collective-permute-start(bf16[1536,768]{1,0:T(8,128)(2,1)S(1)} %copy-done.1), channel_id=1, source_target_pairs={{0,1},{1,0},{2,3},{3,2},{4,5},{5,4},{6,7},{7,6},{8,9},{9,8},{10,11... | collective-permute-start | bytes 7077896 | tf_op jit(solution)/shard_map/ppermute | solution.py:579
  21.9 19.3 %collective-permute-start.9 = (bf16[1536,768]{1,0:T(8,128)(2,1)S(1)}, bf16[1536,768]{1,0:T(8,128)(2,1)S(1)}, u32[]{:S(2)}, u32[]{:S(2)}) collective-permute-start(bf16[1536,768]{1,0:T(8,128)(2,1)S(1)} %copy-done.2), channel_id=1, source_target_pairs={{0,1},{1,0},{2,3},{3,2},{4,5},{5,4},{6,7},{7,6},{8,9},{9,8},{10,11... | collective-permute-start | bytes 7077896 | tf_op jit(solution)/shard_map/ppermute | solution.py:579
  58.2 17.4 %collective-permute-start.15 = (bf16[384,1536]{1,0:T(8,128)(2,1)}, bf16[384,1536]{1,0:T(8,128)(2,1)S(1)}, u32[]{:S(2)}, u32[]{:S(2)}) collective-permute-start(bf16[384,1536]{1,0:T(8,128)(2,1)} %get-tuple-element.101), channel_id=1, source_target_pairs={{0,1},{1,0},{2,3},{3,2},{4,5},{5,4},{6,7},{7,6},{8,9},{9,8},{10,11... | collective-permute-start | bytes 3538952 | tf_op jit(solution)/shard_map/ppermute | solution.py:579
  58.8 24.6 %collective-permute-start.10 = (bf16[3,1,144,768]{3,2,1,0:T(8,128)(2,1)S(1)}, bf16[3,1,144,768]{3,2,1,0:T(8,128)(2,1)}, u32[]{:S(2)}, u32[]{:S(2)}) collective-permute-start(bf16[3,1,144,768]{3,2,1,0:T(8,128)(2,1)S(1)} %bitcast.60), channel_id=1, source_target_pairs={{0,2},{1,5},{2,0},{3,7},{4,6},{5,1},{6,4},{7,3},{8,10},{9,13},{10,... | collective-permute-start | bytes 1990664 | tf_op jit(solution)/shard_map/ppermute | solution.py:587
  63.4 20.0 %collective-permute-start.11 = (bf16[3,1,144,768]{3,2,1,0:T(8,128)(2,1)S(1)}, bf16[3,1,144,768]{3,2,1,0:T(8,128)(2,1)}, u32[]{:S(2)}, u32[]{:S(2)}) collective-permute-start(bf16[3,1,144,768]{3,2,1,0:T(8,128)(2,1)S(1)} %bitcast.61), channel_id=1, source_target_pairs={{0,4},{1,3},{2,6},{3,1},{4,0},{5,7},{6,2},{7,5},{8,12},{9,11},{10,... | collective-permute-start | bytes 1990664 | tf_op jit(solution)/shard_map/ppermute | solution.py:587
  66.4 18.9 %collective-permute-start.16 = (bf16[3,144,768]{2,1,0:T(8,128)(2,1)S(1)}, bf16[3,144,768]{2,1,0:T(8,128)(2,1)S(1)}, u32[]{:S(2)}, u32[]{:S(2)}) collective-permute-start(bf16[3,144,768]{2,1,0:T(8,128)(2,1)S(1)} %get-tuple-element.93.refs_1_.d_attn_a), channel_id=1, source_target_pairs={{0,1},{1,0},{2,3},{3,2},{4,5},{5,4},{6,7},{7,6},{8,9},{9,8},{10,11... | collective-permute-start | bytes 1990664 | tf_op jit(solution)/shard_map/ppermute | solution.py:579
  73.9 20.9 %collective-permute-start.17 = (bf16[2,192,1536]{2,1,0:T(8,128)(2,1)}, bf16[2,192,1536]{2,1,0:T(8,128)(2,1)S(1)}, u32[]{:S(2)}, u32[]{:S(2)}) collective-permute-start(bf16[2,192,1536]{2,1,0:T(8,128)(2,1)} %get-tuple-element.98), channel_id=1, source_target_pairs={{0,2},{1,5},{2,0},{3,7},{4,6},{5,1},{6,4},{7,3},{8,10},{9,13},{10,... | collective-permute-start | bytes 3538952 | tf_op jit(solution)/shard_map/ppermute | solution.py:587
  83.4 19.7 %collective-permute-start.20 = (bf16[3,1,144,768]{3,2,1,0:T(8,128)(2,1)}, bf16[3,1,144,768]{3,2,1,0:T(8,128)(2,1)}, u32[]{:S(2)}, u32[]{:S(2)}) collective-permute-start(bf16[3,1,144,768]{3,2,1,0:T(8,128)(2,1)} %collective-permute-done.10.refs_9_), channel_id=1, source_target_pairs={{0,4},{1,3},{2,6},{3,1},{4,0},{5,7},{6,2},{7,5},{8,12},{9,11},{10,... | collective-permute-start | bytes 1990664 | tf_op jit(solution)/shard_map/ppermute | solution.py:587
  84.8 28.7 %collective-permute-start.22 = (bf16[3,1,144,768]{3,2,1,0:T(8,128)(2,1)}, bf16[3,1,144,768]{3,2,1,0:T(8,128)(2,1)}, u32[]{:S(2)}, u32[]{:S(2)}) collective-permute-start(bf16[3,1,144,768]{3,2,1,0:T(8,128)(2,1)} %collective-permute-done.10.refs_9_), channel_id=1, source_target_pairs={{0,1},{1,0},{2,3},{3,2},{4,5},{5,4},{6,7},{7,6},{8,9},{9,8},{10,11... | collective-permute-start | bytes 1990664 | tf_op jit(solution)/shard_map/ppermute | solution.py:579
  84.8 23.5 %collective-permute-start.21 = (bf16[3,1,144,768]{3,2,1,0:T(8,128)(2,1)}, bf16[3,1,144,768]{3,2,1,0:T(8,128)(2,1)}, u32[]{:S(2)}, u32[]{:S(2)}) collective-permute-start(bf16[3,1,144,768]{3,2,1,0:T(8,128)(2,1)} %collective-permute-done.11.refs_10_), channel_id=1, source_target_pairs={{0,1},{1,0},{2,3},{3,2},{4,5},{5,4},{6,7},{7,6},{8,9},{9,8},{10,11... | collective-permute-start | bytes 1990664 | tf_op jit(solution)/shard_map/ppermute | solution.py:579
  103.1 20.7 %collective-permute-start.26 = (bf16[2,192,1536]{2,1,0:T(8,128)(2,1)}, bf16[2,192,1536]{2,1,0:T(8,128)(2,1)S(1)}, u32[]{:S(2)}, u32[]{:S(2)}) collective-permute-start(bf16[2,192,1536]{2,1,0:T(8,128)(2,1)} %get-tuple-element.103), channel_id=1, source_target_pairs={{0,2},{1,5},{2,0},{3,7},{4,6},{5,1},{6,4},{7,3},{8,10},{9,13},{10,... | collective-permute-start | bytes 3538952 | tf_op jit(solution)/shard_map/ppermute | solution.py:587
  105.6 23.2 %collective-permute-start.24 = (bf16[2,208,768]{2,1,0:T(8,128)(2,1)}, bf16[2,208,768]{2,1,0:T(8,128)(2,1)S(1)}, u32[]{:S(2)}, u32[]{:S(2)}) collective-permute-start(bf16[2,208,768]{2,1,0:T(8,128)(2,1)} %get-tuple-element.111), channel_id=1, source_target_pairs={{0,2},{1,5},{2,0},{3,7},{4,6},{5,1},{6,4},{7,3},{8,10},{9,13},{10,... | collective-permute-start | bytes 1916936 | tf_op jit(solution)/shard_map/ppermute | solution.py:587
  108.3 16.8 %collective-permute-start.25 = (bf16[96,1536]{1,0:T(8,128)(2,1)S(1)}, bf16[96,1536]{1,0:T(8,128)(2,1)S(1)}, u32[]{:S(2)}, u32[]{:S(2)}) collective-permute-start(bf16[96,1536]{1,0:T(8,128)(2,1)S(1)} %fusion.9), channel_id=1, source_target_pairs={{0,8},{8,0},{16,24},{24,16},{1,9},{9,1},{17,25},{25,17},{2,10},{10... | collective-permute-start | bytes 884744 | tf_op jit(solution)/shard_map/ppermute | solution.py:845
  124.0 18.3 %collective-permute-start.33 = (bf16[1,192,1536]{2,1,0:T(8,128)(2,1)S(1)}, bf16[1,192,1536]{2,1,0:T(8,128)(2,1)S(1)}, u32[]{:S(2)}, u32[]{:S(2)}) collective-permute-start(bf16[1,192,1536]{2,1,0:T(8,128)(2,1)S(1)} %add_convert_fusion), channel_id=1, source_target_pairs={{0,4},{1,3},{2,6},{3,1},{4,0},{5,7},{6,2},{7,5},{8,12},{9,11},{10,... | collective-permute-start | bytes 1769480 | tf_op jit(solution)/shard_map/ppermute | solution.py:587
  128.9 22.6 %collective-permute-start.30 = (bf16[1,208,768]{2,1,0:T(8,128)(2,1)S(1)}, bf16[1,208,768]{2,1,0:T(8,128)(2,1)S(1)}, u32[]{:S(2)}, u32[]{:S(2)}) collective-permute-start(bf16[1,208,768]{2,1,0:T(8,128)(2,1)S(1)} %add_convert_fusion.2), channel_id=1, source_target_pairs={{0,4},{1,3},{2,6},{3,1},{4,0},{5,7},{6,2},{7,5},{8,12},{9,11},{10,... | collective-permute-start | bytes 958472 | tf_op jit(solution)/shard_map/ppermute | solution.py:587
  129.0 19.2 %collective-permute-start.32 = (bf16[96,1536]{1,0:T(8,128)(2,1)S(1)}, bf16[96,1536]{1,0:T(8,128)(2,1)S(1)}, u32[]{:S(2)}, u32[]{:S(2)}) collective-permute-start(bf16[96,1536]{1,0:T(8,128)(2,1)S(1)} %fusion.6), channel_id=1, source_target_pairs={{0,16},{8,24},{16,0},{24,8},{1,17},{9,25},{17,1},{25,9},{2,18},{10... | collective-permute-start | bytes 884744 | tf_op jit(solution)/shard_map/ppermute | solution.py:845
  142.3 54.4 %collective-permute-start.27 = (bf16[3,128,768]{2,1,0:T(8,128)(2,1)S(1)}, bf16[3,128,768]{2,1,0:T(8,128)(2,1)S(1)}, u32[]{:S(2)}, u32[]{:S(2)}) collective-permute-start(bf16[3,128,768]{2,1,0:T(8,128)(2,1)S(1)} %copy-done.23), channel_id=1, source_target_pairs={{0,1},{1,0},{2,3},{3,2},{4,5},{5,4},{6,7},{7,6},{8,9},{9,8},{10,11... | collective-permute-start | bytes 1769480 | tf_op jit(solution)/shard_map/ppermute | solution.py:579
  142.3 56.5 %collective-permute-start.28 = (f32[3,128,768]{2,1,0:T(8,128)S(1)}, f32[3,128,768]{2,1,0:T(8,128)S(1)}, u32[]{:S(2)}, u32[]{:S(2)}) collective-permute-start(f32[3,128,768]{2,1,0:T(8,128)S(1)} %copy-done.21), channel_id=1, source_target_pairs={{0,1},{1,0},{2,3},{3,2},{4,5},{5,4},{6,7},{7,6},{8,9},{9,8},{10,11... | collective-permute-start | bytes 3538952 | tf_op jit(solution)/shard_map/ppermute | solution.py:579
  148.2 50.6 %collective-permute-start.29 = (bf16[3,256,768]{2,1,0:T(8,128)(2,1)S(1)}, bf16[3,256,768]{2,1,0:T(8,128)(2,1)S(1)}, u32[]{:S(2)}, u32[]{:S(2)}) collective-permute-start(bf16[3,256,768]{2,1,0:T(8,128)(2,1)S(1)} %get-tuple-element.131), channel_id=1, source_target_pairs={{0,1},{1,0},{2,3},{3,2},{4,5},{5,4},{6,7},{7,6},{8,9},{9,8},{10,11... | collective-permute-start | bytes 3538952 | tf_op jit(solution)/shard_map/ppermute | solution.py:579
  151.5 13.3 %collective-permute-start.44 = (bf16[96,1536]{1,0:T(8,128)(2,1)S(1)}, bf16[96,1536]{1,0:T(8,128)(2,1)S(1)}, u32[]{:S(2)}, u32[]{:S(2)}) collective-permute-start(bf16[96,1536]{1,0:T(8,128)(2,1)S(1)} %add_convert_fusion.5), channel_id=1, source_target_pairs={{0,8},{8,0},{16,24},{24,16},{1,9},{9,1},{17,25},{25,17},{2,10},{10... | collective-permute-start | bytes 884744 | tf_op jit(solution)/shard_map/ppermute | solution.py:845
  167.7 12.5 %collective-permute-start.39 = (bf16[96,1536]{1,0:T(8,128)(2,1)S(1)}, bf16[96,1536]{1,0:T(8,128)(2,1)S(1)}, u32[]{:S(2)}, u32[]{:S(2)}) collective-permute-start(bf16[96,1536]{1,0:T(8,128)(2,1)S(1)} %fusion.5), channel_id=1, source_target_pairs={{0,16},{8,24},{16,0},{24,8},{1,17},{9,25},{17,1},{25,9},{2,18},{10... | collective-permute-start | bytes 884744 | tf_op jit(solution)/shard_map/ppermute | solution.py:845
  182.0 21.6 %collective-permute-start.43 = (bf16[96,1536]{1,0:T(8,128)(2,1)S(1)}, bf16[96,1536]{1,0:T(8,128)(2,1)S(1)}, u32[]{:S(2)}, u32[]{:S(2)}) collective-permute-start(bf16[96,1536]{1,0:T(8,128)(2,1)S(1)} %add_convert_fusion.3), channel_id=1, source_target_pairs={{0,8},{8,0},{16,24},{24,16},{1,9},{9,1},{17,25},{25,17},{2,10},{10... | collective-permute-start | bytes 884744 | tf_op jit(solution)/shard_map/ppermute | solution.py:845
  (58 other events, 494.8 us)

commit v2 on v1

--- a/solution.py
+++ b/solution.py
@@ -8,7 +8,8 @@
 
 HEAD_DIM = 64
 LANES = 128
-STAT_ROWS = 16
+STAT_ROWS = 8
+SMALL_ROWS = 16
 BIG = 2.0**30
 low, full = jnp.bfloat16, jnp.float32
 
@@ -371,7 +372,7 @@
     targets, (turned, slots, turned_second, slots_second) = refs[:-4], refs[-4:]
     span, local = d_query.shape[1:]
     half = span // 2
-    block = targets[0].shape[1] - STAT_ROWS
+    block = targets[0].shape[1] - SMALL_ROWS
     put_slots(turned, slots, [lane_part(part, half) for part in (tok_a, tok_b)], owners, block)
     first = dot_nn(slots[...], both_rows(d_query, half)).astype(low)
     put_slots(turned_second, slots_second, [lane_part(part, half) for part in (d_attn_a, d_attn_b)], owners, block)
@@ -381,9 +382,9 @@
         start = slot * padded(block)
         for which, product in enumerate((first, second)):
             columns = slice(which * local, (which + 1) * local)
-            ref[index, STAT_ROWS:, columns] = product[start : start + block]
-        ref[index, :STAT_ROWS, :local] = jnp.zeros((STAT_ROWS, local), low)
-        ref[index, :STAT_ROWS, local:] = small[owners[slot]].astype(low)
+            ref[index, SMALL_ROWS:, columns] = product[start : start + block]
+        ref[index, :SMALL_ROWS, :local] = jnp.zeros((SMALL_ROWS, local), low)
+        ref[index, :SMALL_ROWS, local:] = small[owners[slot]].astype(low)
 
 
 def key_value_grad_kernel(owners, tok_a, tok_b, d_kv, *refs):
@@ -920,14 +921,14 @@
         )
 
     small_rows = (small[:4] + swap(small)[:4]).reshape(4, ctx_size, quarter).transpose(1, 0, 2)
-    small_rows = jnp.pad(small_rows, ((0, 0), (0, STAT_ROWS - 4), (0, local_width - quarter)))
+    small_rows = jnp.pad(small_rows, ((0, 0), (0, SMALL_ROWS - 4), (0, local_width - quarter)))
     latest = down.advance(d_query)
     d_query, latest = tie(d_query, latest)
     query_out = sequence_grad(
         query_out_grad_kernel,
         (tok_a, tok_b, d_query, payload, payload_b, mixed_keep, mixed_send, small_rows),
         2,
-        STAT_ROWS,
+        SMALL_ROWS,
         2 * local_width,
         "query_out_grad",
     )
@@ -993,7 +994,7 @@
     down_total, up_total = down.total(), up.total()
     query_out_total, key_value_total = query_out.total(), key_value.total()
     small_total = query_out_total[:4, local_width : local_width + quarter]
-    query_out_total = query_out_total[STAT_ROWS:]
+    query_out_total = query_out_total[SMALL_ROWS:]
     return (
         outputs,
         grad_tokens,

time: 207 us -> 207 us (level)
  waiting for transfers between devices: 64.2 us -> 55.5 us
  starting transfers between devices: 45.2 us -> 51.8 us
  Pallas kernels: 76 us -> 78.6 us
    ppermute x14, starting transfers between devices: 21.8 us -> 27 us  [hop(): return lax.ppermute(value, ('ctx', 'tensor'), moves)]
    ppermute x14, waiting for transfers between devices: 16.5 us -> 11.9 us  [hop(): return lax.ppermute(value, ('ctx', 'tensor'), moves)]
    ppermute x12, waiting for transfers between devices: 42.3 us -> 39.7 us  [send(): self.got = lax.ppermute(self.sent, 'dp', moves)]
  transfers between devices with their start and end apart: 45 -> 45, of which waited for: 17 -> 14; matrix products, arithmetic and copies ran while one was open for 6% -> 6% of each run, Pallas kernels for 30% -> 31%
where the time goes in v2:
time: 207 us; the launch traced here: 206 us
  Pallas kernels  78.6 us (38%)
  waiting for transfers between devices  55.5 us (27%)
  starting transfers between devices  51.8 us (25%)
  other arithmetic  12.8 us (6%)
  local copies, waits for them, and re-layouts  6.32 us (3%)
    ppermute x12, waiting for transfers between devices, send(): self.got = lax.ppermute(self.sent, 'dp', moves)  39.7 us
    ppermute x14, starting transfers between devices, hop(): return lax.ppermute(value, ('ctx', 'tensor'), moves)  27 us
    ppermute x12, starting transfers between devices, send(): self.got = lax.ppermute(self.sent, 'dp', moves)  19.5 us
    pallas_call x1, Pallas kernels, on_device(): pl.pallas_call(functools.partial(middle_kernel, min(512, units_local)), g...  14.4 us
    pallas_call x2, Pallas kernels, pair_grad(): pl.pallas_call(pair_grad_kernel, grid_spec=pltpu.PrefetchScalarGridSpec(n...  13.4 us
    ppermute x14, waiting for transfers between devices, hop(): return lax.ppermute(value, ('ctx', 'tensor'), moves)  11.9 us
    pallas_call x1, Pallas kernels, on_device(): pl.pallas_call(functools.partial(key_grad_kernel, counts, heads), grid_sp...  11.7 us
    pallas_call x2, Pallas kernels, sequence_grad(): pl.pallas_call(kernel, grid_spec=pltpu.PrefetchScalarGridSpec(num_scalar_...  11.2 us
  transfers between devices with their start and end apart: 45, of which 14 were waited for; matrix products, arithmetic and copies ran while one was open for 6% of the time, Pallas kernels for 31%

profile of v2, /device:TPU:0, one launch (start us, length us, event | category | flops | bytes accessed | tf_op | source)
XLA Modules:
  0.0 206.2 jit_solution(974915570029779914)
XLA Ops:
  2.8 3.0 %collective-permute-start = (bf16[3,1,136,768]{3,2,0,1:T(8,128)(2,1)S(1)}, bf16[3,1,136,768]{3,2,0,1:T(8,128)(2,1)S(1)}, u32[]{:S(2)}, u32[]{:S(2)}) collective-permute-start(bf16[3,1,136,768]{3,2,0,1:T(8,128)(2,1)S(1)} %get-tuple-element.158), channel_id=1, source_target_pairs={{0,2},{1,5},{2,0},{3,7},{4,6},{5,1},{6,4},{7,3},{8,10},{9,13},{10,... | collective-permute-start | bytes 1880072 | tf_op jit(solution)/shard_map/ppermute | solution.py:588
  10.7 2.4 %attend.3 = (f32[3,384,256]{2,1,0:T(8,128)S(1)}, f32[3,16,256]{2,1,0:T(8,128)S(1)}) custom-call(bf16[3,1,256,1280]{3,2,1,0:T(8,128)(2,1)S(1)} %project.4.refs_0_), custom_call_target="tpu_custom_call" | custom-call | flops 3449999872 | tf_op jit(solution)/shard_map/attend/pallas_call | solution.py:669
  13.1 7.2 %collective-permute-done = bf16[3,1,136,768]{3,2,0,1:T(8,128)(2,1)S(1)} collective-permute-done((bf16[3,1,136,768]{3,2,0,1:T(8,128)(2,1)S(1)}, bf16[3,1,136,768]{3,2,0,1:T(8,128)(2,1)S(1)}, u32[]{:S(2)}, u32[]{:S(2)}) %collective-permute-start) | collective-permute-done | bytes 626720 | tf_op jit(solution)/shard_map/ppermute | solution.py:588
  27.6 3.9 %attend.4 = (f32[3,384,256]{2,1,0:T(8,128)S(1)}, f32[3,16,256]{2,1,0:T(8,128)S(1)}) custom-call(bf16[3,1,256,1280]{3,2,1,0:T(8,128)(2,1)S(1)} %project.4.refs_0_, bf16[3,1,256,1280]{3,2,1,0:T(8,128)(2,1)S(1)} %project.5.refs_1_.refs_4_.refs_6_, bf16[3,1,256,1280]{3,2,1,0:T(8,128)(2,1)S(1)} %project.6.refs_2_.refs_5_.refs_7_, ...), custom_call_target="tpu_custom_call" | custom-call | flops 3449999872 | tf_op jit(solution)/shard_map/attend/pallas_call | solution.py:669
  42.2 14.4 %middle.1 = (bf16[3,128,768]{2,1,0:T(8,128)(2,1)}, f32[3,128,768]{2,1,0:T(8,128)}, bf16[3,136,768]{2,1,0:T(8,128)(2,1)S(1)}, bf16[384,1536]{1,0:T(8,128)(2,1)}, ...) custom-call(s32[1]{0:T(128)} %bitcast.turn_ref, ...), custom_call_target="tpu_custom_call" | custom-call | flops 18400000000 | tf_op jit(solution)/shard_map/middle/pallas_call | solution.py:743
  57.6 3.7 %collective-permute-start.10 = (bf16[3,1,136,768]{3,2,1,0:T(8,128)(2,1)S(1)}, bf16[3,1,136,768]{3,2,1,0:T(8,128)(2,1)}, u32[]{:S(2)}, u32[]{:S(2)}) collective-permute-start(bf16[3,1,136,768]{3,2,1,0:T(8,128)(2,1)S(1)} %bitcast.60), channel_id=1, source_target_pairs={{0,2},{1,5},{2,0},{3,7},{4,6},{5,1},{6,4},{7,3},{8,10},{9,13},{10,... | collective-permute-start | bytes 1880072 | tf_op jit(solution)/shard_map/ppermute | solution.py:588
  62.2 2.7 %collective-permute-start.11 = (bf16[3,1,136,768]{3,2,1,0:T(8,128)(2,1)S(1)}, bf16[3,1,136,768]{3,2,1,0:T(8,128)(2,1)}, u32[]{:S(2)}, u32[]{:S(2)}) collective-permute-start(bf16[3,1,136,768]{3,2,1,0:T(8,128)(2,1)S(1)} %bitcast.61), channel_id=1, source_target_pairs={{0,4},{1,3},{2,6},{3,1},{4,0},{5,7},{6,2},{7,5},{8,12},{9,11},{10,... | collective-permute-start | bytes 1880072 | tf_op jit(solution)/shard_map/ppermute | solution.py:588
  67.3 6.7 %grad_down.1 = (bf16[2,192,1536]{2,1,0:T(8,128)(2,1)}, bf16[1,192,1536]{2,1,0:T(8,128)(2,1)}, bf16[1,192,1536]{2,1,0:T(8,128)(2,1)}) custom-call(s32[4]{0:T(128)S(1)} %fusion.19.owners, bf16[384,768]{1,0:T(8,128)(2,1)} %get-tuple-element.95.left_a, bf16[384,768]{1,0:T(8,128)(2,1)} %copy-done.35, bf16[384,1536]{1,0:T(8,128)(2,1)} %get-tuple-element.96.right_a, ...), custom_call_target="tpu_custom_call" | custom-call | flops 6325000192 | tf_op jit(solution)/shard_map/grad_down/pallas_call | solution.py:775
  76.0 6.7 %grad_up.1 = (bf16[2,192,1536]{2,1,0:T(8,128)(2,1)}, bf16[1,192,1536]{2,1,0:T(8,128)(2,1)}, bf16[1,192,1536]{2,1,0:T(8,128)(2,1)}) custom-call(s32[4]{0:T(128)S(1)} %fusion.19.owners, bf16[384,768]{1,0:T(8,128)(2,1)} %get-tuple-element.99.left_a, bf16[384,768]{1,0:T(8,128)(2,1)} %copy-done.36, bf16[384,1536]{1,0:T(8,128)(2,1)} %get-tuple-element.100.right_a, ...), custom_call_target="tpu_custom_call" | custom-call | flops 6325000192 | tf_op jit(solution)/shard_map/grad_up/pallas_call | solution.py:775
  85.4 10.1 %query_grad.1 = (bf16[3,256,384]{2,1,0:T(8,128)(2,1)}, f32[3,256,384]{2,1,0:T(8,128)}, f32[3,256,384]{2,1,0:T(8,128)}) custom-call(bf16[3,1,256,1280]{3,2,1,0:T(8,128)(2,1)S(1)} %copy-done.11, bf16[3,136,768]{2,1,0:T(8,128)(2,1)S(1)} %get-tuple-element.93.refs_1_.d_attn_a, bf16[3,136,768]{2,1,0:T(8,128)(2,1)S(1)} %collective-permute-done.16.refs_2_.d_attn_b, ...), custom_call_target="tpu_custom_call" | custom-call | flops 12650000384 | tf_op jit(solution)/shard_map/query_grad/pallas_call | solution.py:885
  97.5 6.4 %query_out_grad.1 = (bf16[2,208,768]{2,1,0:T(8,128)(2,1)}, bf16[1,208,768]{2,1,0:T(8,128)(2,1)}, bf16[1,208,768]{2,1,0:T(8,128)(2,1)}) custom-call(s32[4]{0:T(128)S(1)} %fusion.19.owners, bf16[3,136,768]{2,1,0:T(8,128)(2,1)} %copy-done, bf16[3,136,768]{2,1,0:T(8,128)(2,1)} %get-tuple-element.156.tok_b, ...), custom_call_target="tpu_custom_call" | custom-call | flops 6325000192 | tf_op jit(solution)/shard_map/query_out_grad/pallas_call | solution.py:907
  108.6 3.0 %collective-permute-start.25 = (bf16[96,1536]{1,0:T(8,128)(2,1)S(1)}, bf16[96,1536]{1,0:T(8,128)(2,1)S(1)}, u32[]{:S(2)}, u32[]{:S(2)}) collective-permute-start(bf16[96,1536]{1,0:T(8,128)(2,1)S(1)} %fusion.9), channel_id=1, source_target_pairs={{0,8},{8,0},{16,24},{24,16},{1,9},{9,1},{17,25},{25,17},{2,10},{10... | collective-permute-start | bytes 884744 | tf_op jit(solution)/shard_map/ppermute | solution.py:846
  111.7 11.7 %key_grad.1 = (bf16[3,256,768]{2,1,0:T(8,128)(2,1)S(1)}, bf16[3,256,768]{2,1,0:T(8,128)(2,1)S(1)}) custom-call(s32[1]{0:T(128)} %bitcast.turn_ref, bf16[3,1,256,1280]{3,2,1,0:T(8,128)(2,1)S(1)} %copy-done.11, bf16[3,256,384]{2,1,0:T(8,128)(2,1)} %get-tuple-element.113.d_query.refs_1_, f32[3,256,384]{2,1,0:T(8,128)} %get-tuple-element.114.refs_2_, ...), custom_call_target="tpu_custom_call" | custom-call | flops 14375000064 | tf_op jit(solution)/shard_map/key_grad/pallas_call | solution.py:942
  123.5 3.7 %collective-permute-start.33 = (bf16[1,192,1536]{2,1,0:T(8,128)(2,1)S(1)}, bf16[1,192,1536]{2,1,0:T(8,128)(2,1)S(1)}, u32[]{:S(2)}, u32[]{:S(2)}) collective-permute-start(bf16[1,192,1536]{2,1,0:T(8,128)(2,1)S(1)} %add_convert_fusion), channel_id=1, source_target_pairs={{0,4},{1,3},{2,6},{3,1},{4,0},{5,7},{6,2},{7,5},{8,12},{9,11},{10,... | collective-permute-start | bytes 1769480 | tf_op jit(solution)/shard_map/ppermute | solution.py:588
  128.9 5.9 %collective-permute-start.32 = (bf16[96,1536]{1,0:T(8,128)(2,1)S(1)}, bf16[96,1536]{1,0:T(8,128)(2,1)S(1)}, u32[]{:S(2)}, u32[]{:S(2)}) collective-permute-start(bf16[96,1536]{1,0:T(8,128)(2,1)S(1)} %fusion.6), channel_id=1, source_target_pairs={{0,16},{8,24},{16,0},{24,8},{1,17},{9,25},{17,1},{25,9},{2,18},{10... | collective-permute-start | bytes 884744 | tf_op jit(solution)/shard_map/ppermute | solution.py:846
  134.8 4.8 %key_value_grad.1 = (bf16[2,192,768]{2,1,0:T(8,128)(2,1)}, bf16[1,192,768]{2,1,0:T(8,128)(2,1)}, bf16[1,192,768]{2,1,0:T(8,128)(2,1)}) custom-call(s32[4]{0:T(128)S(1)} %fusion.19.owners, bf16[3,136,768]{2,1,0:T(8,128)(2,1)} %copy-done, bf16[3,136,768]{2,1,0:T(8,128)(2,1)} %get-tuple-element.156.tok_b, bf16[3,256,768]{2,1,0:T(8,128)(2,1)} %copy-done.19), custom_call_target="tpu_custom_call" | custom-call | flops 6325000192 | tf_op jit(solution)/shard_map/key_value_grad/pallas_call | solution.py:907
  140.6 4.8 %collective-permute-done.32 = bf16[96,1536]{1,0:T(8,128)(2,1)S(1)} collective-permute-done((bf16[96,1536]{1,0:T(8,128)(2,1)S(1)}, bf16[96,1536]{1,0:T(8,128)(2,1)S(1)}, u32[]{:S(2)}, u32[]{:S(2)}) %collective-permute-start.32) | collective-permute-done | bytes 294944 | tf_op jit(solution)/shard_map/ppermute | solution.py:846
  145.5 4.3 %collective-permute-done.31 = bf16[2,192,768]{2,1,0:T(8,128)(2,1)S(1)} collective-permute-done((bf16[2,192,768]{2,1,0:T(8,128)(2,1)}, bf16[2,192,768]{2,1,0:T(8,128)(2,1)S(1)}, u32[]{:S(2)}, u32[]{:S(2)}) %collective-permute-start.31) | collective-permute-done | bytes 589856 | tf_op jit(solution)/shard_map/ppermute | solution.py:588
  152.0 6.1 %collective-permute-done.36 = bf16[96,1536]{1,0:T(8,128)(2,1)S(1)} collective-permute-done((bf16[96,1536]{1,0:T(8,128)(2,1)S(1)}, bf16[96,1536]{1,0:T(8,128)(2,1)S(1)}, u32[]{:S(2)}, u32[]{:S(2)}) %collective-permute-start.36) | collective-permute-done | bytes 294944 | tf_op jit(solution)/shard_map/ppermute | solution.py:846
  166.6 5.7 %collective-permute-done.34 = bf16[104,768]{1,0:T(8,128)(2,1)S(1)} collective-permute-done((bf16[104,768]{1,0:T(8,128)(2,1)S(1)}, bf16[104,768]{1,0:T(8,128)(2,1)S(1)}, u32[]{:S(2)}, u32[]{:S(2)}) %collective-permute-start.34) | collective-permute-done | bytes 159776 | tf_op jit(solution)/shard_map/ppermute | solution.py:846
  172.3 6.8 %collective-permute-done.39 = bf16[96,1536]{1,0:T(8,128)(2,1)S(1)} collective-permute-done((bf16[96,1536]{1,0:T(8,128)(2,1)S(1)}, bf16[96,1536]{1,0:T(8,128)(2,1)S(1)}, u32[]{:S(2)}, u32[]{:S(2)}) %collective-permute-start.39) | collective-permute-done | bytes 294944 | tf_op jit(solution)/shard_map/ppermute | solution.py:846
  180.6 3.6 %collective-permute-start.43 = (bf16[96,1536]{1,0:T(8,128)(2,1)S(1)}, bf16[96,1536]{1,0:T(8,128)(2,1)S(1)}, u32[]{:S(2)}, u32[]{:S(2)}) collective-permute-start(bf16[96,1536]{1,0:T(8,128)(2,1)S(1)} %add_convert_fusion.3), channel_id=1, source_target_pairs={{0,8},{8,0},{16,24},{24,16},{1,9},{9,1},{17,25},{25,17},{2,10},{10... | collective-permute-start | bytes 884744 | tf_op jit(solution)/shard_map/ppermute | solution.py:846
  184.3 4.9 %collective-permute-done.37 = bf16[104,768]{1,0:T(8,128)(2,1)S(1)} collective-permute-done((bf16[104,768]{1,0:T(8,128)(2,1)S(1)}, bf16[104,768]{1,0:T(8,128)(2,1)S(1)}, u32[]{:S(2)}, u32[]{:S(2)}) %collective-permute-start.37) | collective-permute-done | bytes 159776 | tf_op jit(solution)/shard_map/ppermute | solution.py:846
  189.3 7.9 %collective-permute-done.41 = bf16[96,768]{1,0:T(8,128)(2,1)S(1)} collective-permute-done((bf16[96,768]{1,0:T(8,128)(2,1)S(1)}, bf16[96,768]{1,0:T(8,128)(2,1)S(1)}, u32[]{:S(2)}, u32[]{:S(2)}) %collective-permute-start.41) | collective-permute-done | bytes 147488 | tf_op jit(solution)/shard_map/ppermute | solution.py:846
  (191 shorter events, 64.6 us)
Async XLA Ops:
  2.8 17.4 %collective-permute-start = (bf16[3,1,136,768]{3,2,0,1:T(8,128)(2,1)S(1)}, bf16[3,1,136,768]{3,2,0,1:T(8,128)(2,1)S(1)}, u32[]{:S(2)}, u32[]{:S(2)}) collective-permute-start(bf16[3,1,136,768]{3,2,0,1:T(8,128)(2,1)S(1)} %get-tuple-element.158), channel_id=1, source_target_pairs={{0,2},{1,5},{2,0},{3,7},{4,6},{5,1},{6,4},{7,3},{8,10},{9,13},{10,... | collective-permute-start | bytes 1880072 | tf_op jit(solution)/shard_map/ppermute | solution.py:588
  5.8 14.4 %collective-permute-start.1 = (bf16[3,1,136,768]{3,2,0,1:T(8,128)(2,1)S(1)}, bf16[3,1,136,768]{3,2,0,1:T(8,128)(2,1)S(1)}, u32[]{:S(2)}, u32[]{:S(2)}) collective-permute-start(bf16[3,1,136,768]{3,2,0,1:T(8,128)(2,1)S(1)} %get-tuple-element.158), channel_id=1, source_target_pairs={{0,4},{1,3},{2,6},{3,1},{4,0},{5,7},{6,2},{7,5},{8,12},{9,11},{10,... | collective-permute-start | bytes 1880072 | tf_op jit(solution)/shard_map/ppermute | solution.py:588
  20.8 19.7 %collective-permute-start.8 = (bf16[1536,768]{1,0:T(8,128)(2,1)S(1)}, bf16[1536,768]{1,0:T(8,128)(2,1)S(1)}, u32[]{:S(2)}, u32[]{:S(2)}) collective-permute-start(bf16[1536,768]{1,0:T(8,128)(2,1)S(1)} %copy-done.1), channel_id=1, source_target_pairs={{0,1},{1,0},{2,3},{3,2},{4,5},{5,4},{6,7},{7,6},{8,9},{9,8},{10,11... | collective-permute-start | bytes 7077896 | tf_op jit(solution)/shard_map/ppermute | solution.py:580
  21.1 19.3 %collective-permute-start.9 = (bf16[1536,768]{1,0:T(8,128)(2,1)S(1)}, bf16[1536,768]{1,0:T(8,128)(2,1)S(1)}, u32[]{:S(2)}, u32[]{:S(2)}) collective-permute-start(bf16[1536,768]{1,0:T(8,128)(2,1)S(1)} %copy-done.2), channel_id=1, source_target_pairs={{0,1},{1,0},{2,3},{3,2},{4,5},{5,4},{6,7},{7,6},{8,9},{9,8},{10,11... | collective-permute-start | bytes 7077896 | tf_op jit(solution)/shard_map/ppermute | solution.py:580
  57.1 17.8 %collective-permute-start.15 = (bf16[384,1536]{1,0:T(8,128)(2,1)}, bf16[384,1536]{1,0:T(8,128)(2,1)S(1)}, u32[]{:S(2)}, u32[]{:S(2)}) collective-permute-start(bf16[384,1536]{1,0:T(8,128)(2,1)} %get-tuple-element.101), channel_id=1, source_target_pairs={{0,1},{1,0},{2,3},{3,2},{4,5},{5,4},{6,7},{7,6},{8,9},{9,8},{10,11... | collective-permute-start | bytes 3538952 | tf_op jit(solution)/shard_map/ppermute | solution.py:580
  57.6 25.1 %collective-permute-start.10 = (bf16[3,1,136,768]{3,2,1,0:T(8,128)(2,1)S(1)}, bf16[3,1,136,768]{3,2,1,0:T(8,128)(2,1)}, u32[]{:S(2)}, u32[]{:S(2)}) collective-permute-start(bf16[3,1,136,768]{3,2,1,0:T(8,128)(2,1)S(1)} %bitcast.60), channel_id=1, source_target_pairs={{0,2},{1,5},{2,0},{3,7},{4,6},{5,1},{6,4},{7,3},{8,10},{9,13},{10,... | collective-permute-start | bytes 1880072 | tf_op jit(solution)/shard_map/ppermute | solution.py:588
  62.2 20.5 %collective-permute-start.11 = (bf16[3,1,136,768]{3,2,1,0:T(8,128)(2,1)S(1)}, bf16[3,1,136,768]{3,2,1,0:T(8,128)(2,1)}, u32[]{:S(2)}, u32[]{:S(2)}) collective-permute-start(bf16[3,1,136,768]{3,2,1,0:T(8,128)(2,1)S(1)} %bitcast.61), channel_id=1, source_target_pairs={{0,4},{1,3},{2,6},{3,1},{4,0},{5,7},{6,2},{7,5},{8,12},{9,11},{10,... | collective-permute-start | bytes 1880072 | tf_op jit(solution)/shard_map/ppermute | solution.py:588
  66.4 18.9 %collective-permute-start.16 = (bf16[3,136,768]{2,1,0:T(8,128)(2,1)S(1)}, bf16[3,136,768]{2,1,0:T(8,128)(2,1)S(1)}, u32[]{:S(2)}, u32[]{:S(2)}) collective-permute-start(bf16[3,136,768]{2,1,0:T(8,128)(2,1)S(1)} %get-tuple-element.93.refs_1_.d_attn_a), channel_id=1, source_target_pairs={{0,1},{1,0},{2,3},{3,2},{4,5},{5,4},{6,7},{7,6},{8,9},{9,8},{10,11... | collective-permute-start | bytes 1880072 | tf_op jit(solution)/shard_map/ppermute | solution.py:580
  74.0 21.4 %collective-permute-start.17 = (bf16[2,192,1536]{2,1,0:T(8,128)(2,1)}, bf16[2,192,1536]{2,1,0:T(8,128)(2,1)S(1)}, u32[]{:S(2)}, u32[]{:S(2)}) collective-permute-start(bf16[2,192,1536]{2,1,0:T(8,128)(2,1)} %get-tuple-element.98), channel_id=1, source_target_pairs={{0,2},{1,5},{2,0},{3,7},{4,6},{5,1},{6,4},{7,3},{8,10},{9,13},{10,... | collective-permute-start | bytes 3538952 | tf_op jit(solution)/shard_map/ppermute | solution.py:588
  82.7 21.1 %collective-permute-start.20 = (bf16[3,1,136,768]{3,2,1,0:T(8,128)(2,1)}, bf16[3,1,136,768]{3,2,1,0:T(8,128)(2,1)}, u32[]{:S(2)}, u32[]{:S(2)}) collective-permute-start(bf16[3,1,136,768]{3,2,1,0:T(8,128)(2,1)} %collective-permute-done.10.refs_9_), channel_id=1, source_target_pairs={{0,4},{1,3},{2,6},{3,1},{4,0},{5,7},{6,2},{7,5},{8,12},{9,11},{10,... | collective-permute-start | bytes 1880072 | tf_op jit(solution)/shard_map/ppermute | solution.py:588
  84.8 26.9 %collective-permute-start.22 = (bf16[3,1,136,768]{3,2,1,0:T(8,128)(2,1)}, bf16[3,1,136,768]{3,2,1,0:T(8,128)(2,1)}, u32[]{:S(2)}, u32[]{:S(2)}) collective-permute-start(bf16[3,1,136,768]{3,2,1,0:T(8,128)(2,1)} %collective-permute-done.10.refs_9_), channel_id=1, source_target_pairs={{0,1},{1,0},{2,3},{3,2},{4,5},{5,4},{6,7},{7,6},{8,9},{9,8},{10,11... | collective-permute-start | bytes 1880072 | tf_op jit(solution)/shard_map/ppermute | solution.py:580
  84.8 23.8 %collective-permute-start.21 = (bf16[3,1,136,768]{3,2,1,0:T(8,128)(2,1)}, bf16[3,1,136,768]{3,2,1,0:T(8,128)(2,1)}, u32[]{:S(2)}, u32[]{:S(2)}) collective-permute-start(bf16[3,1,136,768]{3,2,1,0:T(8,128)(2,1)} %collective-permute-done.11.refs_10_), channel_id=1, source_target_pairs={{0,1},{1,0},{2,3},{3,2},{4,5},{5,4},{6,7},{7,6},{8,9},{9,8},{10,11... | collective-permute-start | bytes 1880072 | tf_op jit(solution)/shard_map/ppermute | solution.py:580
  103.9 19.4 %collective-permute-start.26 = (bf16[2,192,1536]{2,1,0:T(8,128)(2,1)}, bf16[2,192,1536]{2,1,0:T(8,128)(2,1)S(1)}, u32[]{:S(2)}, u32[]{:S(2)}) collective-permute-start(bf16[2,192,1536]{2,1,0:T(8,128)(2,1)} %get-tuple-element.103), channel_id=1, source_target_pairs={{0,2},{1,5},{2,0},{3,7},{4,6},{5,1},{6,4},{7,3},{8,10},{9,13},{10,... | collective-permute-start | bytes 3538952 | tf_op jit(solution)/shard_map/ppermute | solution.py:588
  106.0 22.5 %collective-permute-start.24 = (bf16[2,208,768]{2,1,0:T(8,128)(2,1)}, bf16[2,208,768]{2,1,0:T(8,128)(2,1)S(1)}, u32[]{:S(2)}, u32[]{:S(2)}) collective-permute-start(bf16[2,208,768]{2,1,0:T(8,128)(2,1)} %get-tuple-element.111), channel_id=1, source_target_pairs={{0,2},{1,5},{2,0},{3,7},{4,6},{5,1},{6,4},{7,3},{8,10},{9,13},{10,... | collective-permute-start | bytes 1916936 | tf_op jit(solution)/shard_map/ppermute | solution.py:588
  108.6 18.6 %collective-permute-start.25 = (bf16[96,1536]{1,0:T(8,128)(2,1)S(1)}, bf16[96,1536]{1,0:T(8,128)(2,1)S(1)}, u32[]{:S(2)}, u32[]{:S(2)}) collective-permute-start(bf16[96,1536]{1,0:T(8,128)(2,1)S(1)} %fusion.9), channel_id=1, source_target_pairs={{0,8},{8,0},{16,24},{24,16},{1,9},{9,1},{17,25},{25,17},{2,10},{10... | collective-permute-start | bytes 884744 | tf_op jit(solution)/shard_map/ppermute | solution.py:846
  123.5 16.4 %collective-permute-start.33 = (bf16[1,192,1536]{2,1,0:T(8,128)(2,1)S(1)}, bf16[1,192,1536]{2,1,0:T(8,128)(2,1)S(1)}, u32[]{:S(2)}, u32[]{:S(2)}) collective-permute-start(bf16[1,192,1536]{2,1,0:T(8,128)(2,1)S(1)} %add_convert_fusion), channel_id=1, source_target_pairs={{0,4},{1,3},{2,6},{3,1},{4,0},{5,7},{6,2},{7,5},{8,12},{9,11},{10,... | collective-permute-start | bytes 1769480 | tf_op jit(solution)/shard_map/ppermute | solution.py:588
  128.6 21.2 %collective-permute-start.30 = (bf16[1,208,768]{2,1,0:T(8,128)(2,1)S(1)}, bf16[1,208,768]{2,1,0:T(8,128)(2,1)S(1)}, u32[]{:S(2)}, u32[]{:S(2)}) collective-permute-start(bf16[1,208,768]{2,1,0:T(8,128)(2,1)S(1)} %add_convert_fusion.2), channel_id=1, source_target_pairs={{0,4},{1,3},{2,6},{3,1},{4,0},{5,7},{6,2},{7,5},{8,12},{9,11},{10,... | collective-permute-start | bytes 958472 | tf_op jit(solution)/shard_map/ppermute | solution.py:588
  128.9 16.5 %collective-permute-start.32 = (bf16[96,1536]{1,0:T(8,128)(2,1)S(1)}, bf16[96,1536]{1,0:T(8,128)(2,1)S(1)}, u32[]{:S(2)}, u32[]{:S(2)}) collective-permute-start(bf16[96,1536]{1,0:T(8,128)(2,1)S(1)} %fusion.6), channel_id=1, source_target_pairs={{0,16},{8,24},{16,0},{24,8},{1,17},{9,25},{17,1},{25,9},{2,18},{10... | collective-permute-start | bytes 884744 | tf_op jit(solution)/shard_map/ppermute | solution.py:846
  139.9 57.6 %collective-permute-start.27 = (bf16[3,128,768]{2,1,0:T(8,128)(2,1)S(1)}, bf16[3,128,768]{2,1,0:T(8,128)(2,1)S(1)}, u32[]{:S(2)}, u32[]{:S(2)}) collective-permute-start(bf16[3,128,768]{2,1,0:T(8,128)(2,1)S(1)} %copy-done.23), channel_id=1, source_target_pairs={{0,1},{1,0},{2,3},{3,2},{4,5},{5,4},{6,7},{7,6},{8,9},{9,8},{10,11... | collective-permute-start | bytes 1769480 | tf_op jit(solution)/shard_map/ppermute | solution.py:580
  140.0 59.3 %collective-permute-start.28 = (f32[3,128,768]{2,1,0:T(8,128)S(1)}, f32[3,128,768]{2,1,0:T(8,128)S(1)}, u32[]{:S(2)}, u32[]{:S(2)}) collective-permute-start(f32[3,128,768]{2,1,0:T(8,128)S(1)} %copy-done.21), channel_id=1, source_target_pairs={{0,1},{1,0},{2,3},{3,2},{4,5},{5,4},{6,7},{7,6},{8,9},{9,8},{10,11... | collective-permute-start | bytes 3538952 | tf_op jit(solution)/shard_map/ppermute | solution.py:580
  145.4 53.9 %collective-permute-start.29 = (bf16[3,256,768]{2,1,0:T(8,128)(2,1)S(1)}, bf16[3,256,768]{2,1,0:T(8,128)(2,1)S(1)}, u32[]{:S(2)}, u32[]{:S(2)}) collective-permute-start(bf16[3,256,768]{2,1,0:T(8,128)(2,1)S(1)} %get-tuple-element.131), channel_id=1, source_target_pairs={{0,1},{1,0},{2,3},{3,2},{4,5},{5,4},{6,7},{7,6},{8,9},{9,8},{10,11... | collective-permute-start | bytes 3538952 | tf_op jit(solution)/shard_map/ppermute | solution.py:580
  149.8 12.3 %collective-permute-start.44 = (bf16[96,1536]{1,0:T(8,128)(2,1)S(1)}, bf16[96,1536]{1,0:T(8,128)(2,1)S(1)}, u32[]{:S(2)}, u32[]{:S(2)}) collective-permute-start(bf16[96,1536]{1,0:T(8,128)(2,1)S(1)} %add_convert_fusion.5), channel_id=1, source_target_pairs={{0,8},{8,0},{16,24},{24,16},{1,9},{9,1},{17,25},{25,17},{2,10},{10... | collective-permute-start | bytes 884744 | tf_op jit(solution)/shard_map/ppermute | solution.py:846
  164.9 14.2 %collective-permute-start.39 = (bf16[96,1536]{1,0:T(8,128)(2,1)S(1)}, bf16[96,1536]{1,0:T(8,128)(2,1)S(1)}, u32[]{:S(2)}, u32[]{:S(2)}) collective-permute-start(bf16[96,1536]{1,0:T(8,128)(2,1)S(1)} %fusion.5), channel_id=1, source_target_pairs={{0,16},{8,24},{16,0},{24,8},{1,17},{9,25},{17,1},{25,9},{2,18},{10... | collective-permute-start | bytes 884744 | tf_op jit(solution)/shard_map/ppermute | solution.py:846
  180.6 23.4 %collective-permute-start.43 = (bf16[96,1536]{1,0:T(8,128)(2,1)S(1)}, bf16[96,1536]{1,0:T(8,128)(2,1)S(1)}, u32[]{:S(2)}, u32[]{:S(2)}) collective-permute-start(bf16[96,1536]{1,0:T(8,128)(2,1)S(1)} %add_convert_fusion.3), channel_id=1, source_target_pairs={{0,8},{8,0},{16,24},{24,16},{1,9},{9,1},{17,25},{25,17},{2,10},{10... | collective-permute-start | bytes 884744 | tf_op jit(solution)/shard_map/ppermute | solution.py:846
  (58 other events, 496.1 us)
